TPU v7x, 32 devices: a whole 2x2x4 slice. The times are simulated.
32 devices in a mesh: gx: 8 (over z, x), gy: 2 (over y), gz: 2 (over core).
Axes of the slice: x: 2, y: 2, z: 4, core: 2. Of those that a mesh axis runs over, the one named last changes fastest.
Arguments:
- state_field: float32 [128, 5, 32, 256], P('gx', None, 'gy', 'gz'), may hold values from -6 to 6
- source: float32 [128, 5, 32, 256], P('gx', None, 'gy', 'gz'), may hold values from -6 to 6
- fluid_mask: int32 [128, 32, 256], P('gx', 'gy', 'gz'), may hold values 0 or 1
- cell_kind: int32 [128, 32, 256], P('gx', 'gy', 'gz'), may hold values from 0 to 2
- boundary_side_number: int32 [128, 32, 256], P('gx', 'gy', 'gz'), may hold values from 0 to 11
- center_matrix: float32 [5, 5], replicated, may hold values from -2.5 to 2.5
- flux_jacobian_blocks: float32 [6, 5, 5], replicated, may hold values from -1 to 1
- wall_matrix: float32 [5, 5], replicated, may hold values from -2.5 to 2.5
- diag_inverse: float32 [128, 5, 5, 32, 256], P('gx', None, None, 'gy', 'gz'), may hold values from -0.01 to 0.1
- lower_coupling: float32 [5, 5], replicated, may hold values from -10 to 10
- upper_neighbour_block: float32 [5, 5], replicated, may hold values from -10 to 10
Outputs:
- update: float32 [128, 5, 32, 256], P('gx', None, 'gy', 'gz')
- residual: float32 [128, 5, 32, 256], P('gx', None, 'gy', 'gz')
Inputs may be any that keep to these rules, and one draw needn't show every extreme that they name: `boundary_side_number`: values 0 to 5 name the face of a cell that is a wall (lower x, upper x, lower y, upper y, lower z, upper z); 6 or more: no wall face. `cell_kind`: 0 full cell, 1 cut cell, 2 small cut cell.
All inputs are finite; a program needn't handle non-finite values. No bound on the sum of `fluid_mask` on one device may be relied on, other than what follows from the above.
Results may differ from a plain program's by a relative error of at most 0.00018.
Values sent between devices are 32-bit elements; how exact they have to be, the bound alone decides.
No kernel may reach another device: no remote copies, remote signals or barrier semaphores. Data moves between devices by JAX's collectives and lax.ppermute only.
A program may use at most 64 MiB of HBM per device.

v0:
```python
import jax
import jax.numpy as jnp
from jax import lax
from jax.sharding import PartitionSpec as P


def with_halo(block, sides, width):
    for axis, dim in sides:
        count = lax.axis_size(axis)
        forward = [(i, i + 1) for i in range(count - 1)]
        backward = [(target, source) for source, target in forward]
        low = lax.ppermute(
            lax.slice_in_dim(block, block.shape[dim] - width, None, axis=dim), axis, forward
        )
        high = lax.ppermute(lax.slice_in_dim(block, 0, width, axis=dim), axis, backward)
        block = jnp.concatenate([low, block, high], axis=dim)
    return block


def const_apply(matrix, vector):
    return jnp.einsum("ab,...byz->...ayz", matrix, vector, precision=lax.Precision.HIGHEST)


def couple(matrix, transfer):
    return jnp.einsum("ab,bcyz->acyz", matrix, transfer, precision=lax.Precision.HIGHEST)


def volume_operator(blocks, vector):
    return jnp.sum(blocks * vector[..., None, :, :, :], axis=-3)


def cell_product(left, right):
    return jnp.sum(left[:, :, None] * right[None], axis=1)


def flux_residual(
    state_field,
    padded,
    source,
    fluid,
    cell_kind,
    boundary_side_number,
    center_matrix,
    flux_jacobian_blocks,
    wall_matrix,
):
    neighbours = [
        padded[:-2, :, 1:-1, 1:-1],
        padded[2:, :, 1:-1, 1:-1],
        padded[1:-1, :, :-2, 1:-1],
        padded[1:-1, :, 2:, 1:-1],
        padded[1:-1, :, 1:-1, :-2],
        padded[1:-1, :, 1:-1, 2:],
    ]
    walled = const_apply(wall_matrix, state_field)
    flux = const_apply(center_matrix, state_field)
    for facing in range(6):
        at_wall = (boundary_side_number == facing)[:, None]
        flux = flux + jnp.where(
            at_wall, walled, const_apply(flux_jacobian_blocks[facing], neighbours[facing])
        )
    weight = jnp.where(cell_kind == 0, 1.0, jnp.where(cell_kind == 1, 2.0, 4.0)).astype(jnp.float32)
    return fluid[:, None] * (source - flux) * weight[:, None]


def pack_maps(transfer, offset):
    comps = offset.shape[0]
    columns = offset.shape[1] * offset.shape[2]
    packed = jnp.concatenate(
        [transfer.reshape(comps * comps, columns), offset.reshape(comps, columns)], axis=0
    )
    return packed[None]


def column_chain(spread, comps, backwards):
    groups = spread.shape[0]
    columns = spread.shape[2]
    matrices = spread[:, : comps * comps].reshape(groups, comps, comps, columns)
    offsets = spread[:, comps * comps :]

    def chain_step(carry, inputs):
        matrix, shift_term = inputs
        following = jnp.sum(matrix * carry[None, :, :], axis=1) + shift_term
        return (following, carry)

    start = jnp.zeros((comps, columns), jnp.float32)
    final, incoming = lax.scan(chain_step, start, (matrices, offsets), reverse=backwards)
    return incoming


def carry_east(transfer, offset):
    spread = lax.all_to_all(
        pack_maps(transfer, offset), "gx", split_axis=2, concat_axis=0, tiled=True
    )
    incoming = column_chain(spread, offset.shape[0], False)
    returned = lax.all_to_all(incoming, "gx", split_axis=0, concat_axis=2, tiled=True)
    return returned.reshape(offset.shape)


def carry_west(transfer, offset):
    spread = lax.all_to_all(
        pack_maps(transfer, offset), "gx", split_axis=2, concat_axis=0, tiled=True
    )
    incoming = column_chain(spread, offset.shape[0], True)
    returned = lax.all_to_all(incoming, "gx", split_axis=0, concat_axis=2, tiled=True)
    return returned.reshape(offset.shape)


def on_device(
    state_field,
    source,
    fluid_mask,
    cell_kind,
    boundary_side_number,
    center_matrix,
    flux_jacobian_blocks,
    wall_matrix,
    diag_inverse,
    lower_coupling,
    upper_neighbour_block,
):
    fluid = fluid_mask.astype(jnp.float32)
    masked = state_field * fluid[:, None]
    padded = with_halo(masked, (("gx", 0), ("gy", 2), ("gz", 3)), 1)
    residual = flux_residual(
        state_field,
        padded,
        source,
        fluid,
        cell_kind,
        boundary_side_number,
        center_matrix,
        flux_jacobian_blocks,
        wall_matrix,
    )
    comps = state_field.shape[1]
    plane_shape = (comps, state_field.shape[2], state_field.shape[3])
    zeroed = jnp.zeros(plane_shape, jnp.float32)
    identity = jnp.broadcast_to(
        jnp.eye(comps, dtype=jnp.float32)[:, :, None, None], (comps, comps) + plane_shape[1:]
    )

    def forward_map(carry, inputs):
        value, transfer = carry
        blocks, term = inputs
        value = volume_operator(blocks, term + const_apply(lower_coupling, value))
        transfer = cell_product(blocks, couple(lower_coupling, transfer))
        return ((value, transfer), None)

    def forward(carry, inputs):
        blocks, term = inputs
        carry = volume_operator(blocks, term + const_apply(lower_coupling, carry))
        return (carry, carry)

    (offset, transfer), unused = lax.scan(forward_map, (zeroed, identity), (diag_inverse, residual))
    incoming = carry_east(transfer, offset)
    final, swept = lax.scan(forward, incoming, (diag_inverse, residual))

    def backward_map(carry, inputs):
        value, transfer = carry
        blocks, term = inputs
        value = term - volume_operator(blocks, const_apply(upper_neighbour_block, value))
        transfer = -cell_product(blocks, couple(upper_neighbour_block, transfer))
        return ((value, transfer), None)

    def backward(carry, inputs):
        blocks, value = inputs
        carry = value - volume_operator(blocks, const_apply(upper_neighbour_block, carry))
        return (carry, carry)

    (offset, transfer), unused = lax.scan(
        backward_map, (zeroed, identity), (diag_inverse, swept), reverse=True
    )
    incoming = carry_west(transfer, offset)
    final, update = lax.scan(backward, incoming, (diag_inverse, swept), reverse=True)
    return (update, residual)


def solution(mesh):
    in_specs = (
        P("gx", None, "gy", "gz"),
        P("gx", None, "gy", "gz"),
        P("gx", "gy", "gz"),
        P("gx", "gy", "gz"),
        P("gx", "gy", "gz"),
        P(),
        P(),
        P(),
        P("gx", None, None, "gy", "gz"),
        P(),
        P(),
    )
    out_specs = (P("gx", None, "gy", "gz"), P("gx", None, "gy", "gz"))
    return jax.shard_map(
        on_device, mesh=mesh, in_specs=in_specs, out_specs=out_specs, check_vma=False
    )
```

profile of v0, /device:TPU:0, one launch (start us, length us, event | category | flops | bytes accessed | tf_op | source)
XLA Modules:
  0.0 266.1 jit_solution(13816744103888163784)
XLA Ops:
  3.2 5.0 %collective-permute-start = (f32[1,5,16,128]{3,1,2,0:T(8,128)S(1)}, f32[1,5,16,128]{3,1,2,0:T(8,128)S(1)}, u32[]{:S(2)}, u32[]{:S(2)}) collective-permute-start(f32[1,5,16,128]{3,1,2,0:T(8,128)S(1)} %get-tuple-element.649), channel_id=1, source_target_pairs={{0,4},{4,8},{8,12},{12,16},{16,20},{20,24},{24,28},{1,5},{5,9},{9,... | collective-permute-start | bytes 122888 | tf_op jit(solution)/shard_map/ppermute | solution.py:12
  11.5 2.2 fusion.37
  14.4 3.4 %collective-permute-start.2 = (f32[18,5,1,128]{3,1,2,0:T(8,128)S(1)}, f32[18,5,1,128]{3,1,2,0:T(8,128)S(1)}, u32[]{:S(2)}, u32[]{:S(2)}) collective-permute-start(f32[18,5,1,128]{3,1,2,0:T(8,128)S(1)} %get-tuple-element.647), channel_id=1, source_target_pairs={{0,2},{1,3},{4,6},{5,7},{8,10},{9,11},{12,14},{13,15},{16,18},{17,... | collective-permute-start | bytes 138248 | tf_op jit(solution)/shard_map/ppermute | solution.py:12
  21.3 2.8 %collective-permute-done.3 = f32[18,5,1,128]{3,1,2,0:T(8,128)S(1)} collective-permute-done((f32[18,5,1,128]{3,1,2,0:T(8,128)S(1)}, f32[18,5,1,128]{3,1,2,0:T(8,128)S(1)}, u32[]{:S(2)}, u32[]{:S(2)}) %collective-permute-start.3) | collective-permute-done | bytes 46112 | tf_op jit(solution)/shard_map/ppermute | solution.py:15
  26.4 2.6 copy.197
  33.6 3.0 %convolution_select_fusion = f32[16,16,128,5]{2,3,1,0:T(8,128)} fusion(f32[16,16,128,5]{2,3,1,0:T(8,128)S(1)} %fusion.35, f32[18,5,1,128]{3,1,2,0:T(8,128)} %copy-done.16, f32[1,5,16,128]{3,1,2,0:T(8,128)} %copy-done.6, f32[16,5,16,128]{3,1,2,0:T(8,128)S(1)} %copy_multiply_fusion, f32[1,5,16,128]{3,1,2,0:T(8,128)S(1)} %collective-permute-done, ...), kind=kOutput, calls=%fused_computation.52 | convolution fusion | flops 10581760 | bytes 2126948 | tf_op jit(solution)/shard_map/ab,...byz->...ayz/dot_general | solution.py:21
  38.8 2.8 %copy.198 = f32[18,5,18,1]{3,1,2,0:T(8,128)} copy(f32[18,5,18,1]{2,3,1,0:T(1,128)} %collective-permute-done.4) | data formatting | bytes 12960 | tf_op jit(solution)/shard_map/ppermute | solution.py:12
  43.4 2.6 convolution_select_fusion.5
  50.1 28.6 %while.87 = (s32[]{:T(128)}, f32[5,16,128]{2,1,0:T(8,128)S(1)}, f32[5,5,16,128]{3,2,1,0:T(8,128)S(1)}, f32[16,5,5,16,128]{4,3,2,1,0:T(8,128)}, f32[16,5,16,128]{...) while((s32[]{:T(128)}, f32[5,16,128]{2,1,0:T(8,128)S(1)}, f32[5,5,16,128]{3,2,1,0:T(8,128)S(1)}, ...), condition=%wide.region_3.4_spmd, body=%wide.region_0.3_spmd.sunk | while | flops 4249602 | bytes 2130205 | solution.py:155
  80.1 9.3 %reduce = f32[2048,30]{1,0:T(8,128)S(1)} reduce(f32[2048,1,30]{2,1,0:T(1,128)S(1)} %bitcast.220, f32[]{:T(128)} %broadcast.68), dimensions={1}, to_apply=%bitcast.170.reduce_sub_computation | reduce | bytes 491524
  91.2 7.0 %all-to-all-start = ((f32[8,1,7680]{2,1,0:T(1,128)}), f32[8,1,7680]{2,1,0:T(1,128)S(1)}, u32[]{:S(2)}, u32[]{:S(2)}) async-start(f32[8,1,7680]{2,1,0:T(1,128)} %reshape.87), calls=%async_computation | async-start | bytes 491520 | tf_op jit(solution)/shard_map/all_to_all | solution.py:92
  98.1 9.7 %all-to-all-done = f32[8,1,7680]{2,1,0:T(1,128)S(1)} async-done(((f32[8,1,7680]{2,1,0:T(1,128)}), f32[8,1,7680]{2,1,0:T(1,128)S(1)}, u32[]{:S(2)}, u32[]{:S(2)}) %all-to-all-start) | async-done | bytes 245792 | tf_op jit(solution)/shard_map/all_to_all | solution.py:92
  111.9 5.7 %while.90 = (s32[]{:T(128)}, f32[5,256]{1,0:T(8,128)S(1)}, f32[8,5,256]{2,1,0:T(8,128)}, f32[8,5,5,256]{3,0,2,1:T(8,128)S(1)}, f32[8,5,256]{2,0,1:T(8,128)S(1)}, /*index=5*/s32[]{:T(128)}, s32[]{:T(128)}) while((s32[]{:T(128)}, f32[5,256]{1,0:T(8,128)S(1)}, f32[8,5,256]{2,1,0:T(8,128)}, f32[8,5,5,256]{3,0,2,1:T(8,128)S(1)}, ...), condition=%wide.region_6.7_spmd.clone, body=%wide.region_4.6_spmd.clone.sunk | while | flops 14083 | bytes 131679 | solution.py:87
  117.6 3.9 %all-to-all-start.1 = ((f32[8,5,256]{2,1,0:T(8,128)}), f32[8,5,256]{2,1,0:T(8,128)S(1)}, u32[]{:S(2)}, u32[]{:S(2)}) async-start(f32[8,5,256]{2,1,0:T(8,128)} %get-tuple-element.444), calls=%async_computation.1 | async-start | bytes 131072 | tf_op jit(solution)/shard_map/all_to_all | solution.py:96
  121.5 6.9 %all-to-all-done.1 = f32[8,5,256]{2,1,0:T(8,128)S(1)} async-done(((f32[8,5,256]{2,1,0:T(8,128)}), f32[8,5,256]{2,1,0:T(8,128)S(1)}, u32[]{:S(2)}, u32[]{:S(2)}) %all-to-all-start.1) | async-done | bytes 40992 | tf_op jit(solution)/shard_map/all_to_all | solution.py:96
  128.5 19.3 %while.88 = (s32[]{:T(128)}, f32[5,16,128]{2,1,0:T(8,128)S(1)}, f32[16,5,16,128]{3,2,1,0:T(8,128)S(1)}, f32[16,5,5,16,128]{4,3,2,1,0:T(8,128)}, f32[16,5,16,128]...) while((s32[]{:T(128)}, f32[5,16,128]{2,1,0:T(8,128)S(1)}, f32[16,5,16,128]{3,2,1,0:T(8,128)S(1)}, ...), condition=%wide.region_9.10_spmd, body=%wide.region_7.9_spmd.sunk | while | flops 716802 | bytes 573629 | solution.py:157
  147.9 29.2 %while.91 = (s32[]{:T(128)}, f32[5,16,128]{2,1,0:T(8,128)S(1)}, f32[5,5,16,128]{3,2,1,0:T(8,128)S(1)}, f32[16,5,16,128]{3,2,1,0:T(8,128)S(1)}, f32[16,5,5,16,128...) while((s32[]{:T(128)}, f32[5,16,128]{2,1,0:T(8,128)S(1)}, ...), condition=%wide.region_13.14_spmd.clone, body=%wide.region_10.13_spmd.clone.sunk | while | flops 4311044 | bytes 2703683 | solution.py:171
  178.7 9.3 %reduce.2 = f32[2048,30]{1,0:T(8,128)S(1)} reduce(f32[2048,1,30]{2,1,0:T(1,128)S(1)} %bitcast.222, f32[]{:T(128)} %broadcast.68), dimensions={1}, to_apply=%bitcast.172.reduce_sub_computation | reduce | bytes 491524
  189.8 3.4 %all-to-all-start.2 = ((f32[8,1,7680]{2,1,0:T(1,128)}), f32[8,1,7680]{2,1,0:T(1,128)S(1)}, u32[]{:S(2)}, u32[]{:S(2)}) async-start(f32[8,1,7680]{2,1,0:T(1,128)} %reshape.89), calls=%async_computation.2 | async-start | bytes 491520 | tf_op jit(solution)/shard_map/all_to_all | solution.py:101
  193.2 8.0 %all-to-all-done.2 = f32[8,1,7680]{2,1,0:T(1,128)S(1)} async-done(((f32[8,1,7680]{2,1,0:T(1,128)}), f32[8,1,7680]{2,1,0:T(1,128)S(1)}, u32[]{:S(2)}, u32[]{:S(2)}) %all-to-all-start.2) | async-done | bytes 245792 | tf_op jit(solution)/shard_map/all_to_all | solution.py:101
  205.3 5.6 %while.92 = (s32[]{:T(128)}, f32[5,256]{1,0:T(8,128)S(1)}, f32[8,5,256]{2,1,0:T(8,128)}, f32[8,5,5,256]{3,0,2,1:T(8,128)S(1)}, f32[8,5,256]{2,0,1:T(8,128)S(1)}, /*index=5*/s32[]{:T(128)}, s32[]{:T(128)}, s32[]{:T(128)}) while((s32[]{:T(128)}, f32[5,256]{1,0:T(8,128)S(1)}, f32[8,5,256]{2,1,0:T(8,128)}, ...), condition=%wide.region_16.17_spmd.clone, body=%wide.region_14.16_spmd.clone.sunk | while | flops 14084 | bytes 131191 | solution.py:87
  211.0 3.4 %all-to-all-start.3 = ((f32[8,5,256]{2,1,0:T(8,128)}), f32[8,5,256]{2,1,0:T(8,128)S(1)}, u32[]{:S(2)}, u32[]{:S(2)}) async-start(f32[8,5,256]{2,1,0:T(8,128)} %get-tuple-element.448), calls=%async_computation.3 | async-start | bytes 131072 | tf_op jit(solution)/shard_map/all_to_all | solution.py:105
  215.3 5.9 %all-to-all-done.3 = f32[8,5,256]{2,1,0:T(8,128)S(1)} async-done(((f32[8,5,256]{2,1,0:T(8,128)}), f32[8,5,256]{2,1,0:T(8,128)S(1)}, u32[]{:S(2)}, u32[]{:S(2)}) %all-to-all-start.3) | async-done | bytes 40992 | tf_op jit(solution)/shard_map/all_to_all | solution.py:105
  221.3 44.0 %while.89 = (s32[]{:T(128)}, f32[5,16,128]{2,1,0:T(8,128)S(1)}, f32[16,5,16,128]{3,2,1,0:T(8,128)S(1)}, f32[16,5,16,128]{3,2,1,0:T(8,128)}, f32[16,5,5,16,128]{4...) while((s32[]{:T(128)}, f32[5,16,128]{2,1,0:T(8,128)S(1)}, ...), condition=%wide.region_19.20_spmd, body=%wide.region_17.19_spmd.sunk | while | flops 727043 | bytes 696529 | solution.py:175
  (584 shorter events, 169.7 us)
Async XLA Ops:
  0.6 8.8 %copy-start = (f32[5,5]{1,0:T(8,128)S(1)}, f32[5,5]{1,0:T(8,128)}, u32[]{:S(2)}) copy-start(f32[5,5]{1,0:T(8,128)} %param.30) | copy-start | bytes 304
  0.6 8.8 %copy-start.1 = (f32[16,5,16,128]{3,2,1,0:T(8,128)S(1)}, f32[16,5,16,128]{3,2,1,0:T(8,128)}, u32[]{:S(2)}) copy-start(f32[16,5,16,128]{3,2,1,0:T(8,128)} %param.23) | copy-start | bytes 1966084
  1.6 9.1 %copy-start.11 = (f32[16,16,128]{2,1,0:T(8,128)}, f32[16,16,128]{2,1,0:T(8,128)S(1)}, u32[]{:S(2)}) copy-start(f32[16,16,128]{2,1,0:T(8,128)S(1)} %convert_element_type.13) | copy-start | bytes 393220
  3.1 7.6 %copy-start.24 = (s32[16,16,128]{2,1,0:T(8,128)S(1)}, s32[16,16,128]{2,1,0:T(8,128)}, u32[]{:S(2)}) copy-start(s32[16,16,128]{2,1,0:T(8,128)} %param.27) | copy-start | bytes 393220
  3.1 8.4 %copy-start.26 = (f32[6,5,5]{2,0,1:T(8,128)S(1)}, f32[6,5,5]{2,0,1:T(8,128)}, u32[]{:S(2)}) copy-start(f32[6,5,5]{2,0,1:T(8,128)} %param.29) | copy-start | bytes 1804
  3.1 8.4 %copy-start.27 = (f32[5,5]{1,0:T(8,128)S(1)}, f32[5,5]{1,0:T(8,128)}, u32[]{:S(2)}) copy-start(f32[5,5]{1,0:T(8,128)} %param.28) | copy-start | bytes 304
  3.2 11.2 %collective-permute-start = (f32[1,5,16,128]{3,1,2,0:T(8,128)S(1)}, f32[1,5,16,128]{3,1,2,0:T(8,128)S(1)}, u32[]{:S(2)}, u32[]{:S(2)}) collective-permute-start(f32[1,5,16,128]{3,1,2,0:T(8,128)S(1)} %get-tuple-element.649), channel_id=1, source_target_pairs={{0,4},{4,8},{8,12},{12,16},{16,20},{20,24},{24,28},{1,5},{5,9},{9,... | collective-permute-start | bytes 122888 | tf_op jit(solution)/shard_map/ppermute | solution.py:12
  8.2 6.2 %collective-permute-start.1 = (f32[1,5,16,128]{3,1,2,0:T(8,128)S(1)}, f32[1,5,16,128]{3,1,2,0:T(8,128)S(1)}, u32[]{:S(2)}, u32[]{:S(2)}) collective-permute-start(f32[1,5,16,128]{3,1,2,0:T(8,128)S(1)} %get-tuple-element.650), channel_id=1, source_target_pairs={{4,0},{8,4},{12,8},{16,12},{20,16},{24,20},{28,24},{5,1},{9,5},{13... | collective-permute-start | bytes 122888 | tf_op jit(solution)/shard_map/ppermute | solution.py:15
  10.7 3.0 %copy-start.25 = (s32[16,16,128]{2,1,0:T(8,128)S(1)}, s32[16,16,128]{2,1,0:T(8,128)}, u32[]{:S(2)}) copy-start(s32[16,16,128]{2,1,0:T(8,128)} %param.26) | copy-start | bytes 393220
  14.4 9.7 %copy-start.6 = (f32[1,5,16,128]{3,1,2,0:T(8,128)}, f32[1,5,16,128]{3,1,2,0:T(8,128)S(1)}, u32[]{:S(2)}) copy-start(f32[1,5,16,128]{3,1,2,0:T(8,128)S(1)} %collective-permute-done.1) | copy-start | bytes 122884
  14.4 6.9 %collective-permute-start.2 = (f32[18,5,1,128]{3,1,2,0:T(8,128)S(1)}, f32[18,5,1,128]{3,1,2,0:T(8,128)S(1)}, u32[]{:S(2)}, u32[]{:S(2)}) collective-permute-start(f32[18,5,1,128]{3,1,2,0:T(8,128)S(1)} %get-tuple-element.647), channel_id=1, source_target_pairs={{0,2},{1,3},{4,6},{5,7},{8,10},{9,11},{12,14},{13,15},{16,18},{17,... | collective-permute-start | bytes 138248 | tf_op jit(solution)/shard_map/ppermute | solution.py:12
  17.9 6.2 %collective-permute-start.3 = (f32[18,5,1,128]{3,1,2,0:T(8,128)S(1)}, f32[18,5,1,128]{3,1,2,0:T(8,128)S(1)}, u32[]{:S(2)}, u32[]{:S(2)}) collective-permute-start(f32[18,5,1,128]{3,1,2,0:T(8,128)S(1)} %get-tuple-element.648), channel_id=1, source_target_pairs={{2,0},{3,1},{6,4},{7,5},{10,8},{11,9},{14,12},{15,13},{18,16},{19,... | collective-permute-start | bytes 138248 | tf_op jit(solution)/shard_map/ppermute | solution.py:15
  21.3 2.8 %copy-start.13 = (f32[18,5,1,128]{3,1,2,0:T(8,128)}, f32[18,5,1,128]{3,1,2,0:T(8,128)S(1)}, u32[]{:S(2)}) copy-start(f32[18,5,1,128]{3,1,2,0:T(8,128)S(1)} %collective-permute-done.2) | copy-start | bytes 138244
  28.9 9.9 %collective-permute-start.4 = (f32[18,5,18,1]{2,3,1,0:T(1,128)}, f32[18,5,18,1]{2,3,1,0:T(1,128)}, u32[]{:S(2)}, u32[]{:S(2)}) collective-permute-start(f32[18,5,18,1]{2,3,1,0:T(1,128)} %copy.197), channel_id=1, source_target_pairs={{0,1},{2,3},{4,5},{6,7},{8,9},{10,11},{12,13},{14,15},{16,17},{18,... | collective-permute-start | bytes 19448 | tf_op jit(solution)/shard_map/ppermute | solution.py:12
  32.1 9.6 %collective-permute-start.5 = (f32[18,5,18,1]{2,3,1,0:T(1,128)}, f32[18,5,18,1]{2,3,1,0:T(1,128)}, u32[]{:S(2)}, u32[]{:S(2)}) collective-permute-start(f32[18,5,18,1]{2,3,1,0:T(1,128)} %copy.200), channel_id=1, source_target_pairs={{1,0},{3,2},{5,4},{7,6},{9,8},{11,10},{13,12},{15,14},{17,16},{19,... | collective-permute-start | bytes 19448 | tf_op jit(solution)/shard_map/ppermute | solution.py:15
  33.6 3.1 %copy-start.7 = (f32[1,5,16,128]{3,1,2,0:T(8,128)S(1)}, f32[1,5,16,128]{3,1,2,0:T(8,128)}, u32[]{:S(2)}) copy-start(f32[1,5,16,128]{3,1,2,0:T(8,128)} %copy-done.6) | copy-start | bytes 122884
  33.6 3.1 %copy-start.14 = (f32[18,5,1,128]{3,1,2,0:T(8,128)S(1)}, f32[18,5,1,128]{3,1,2,0:T(8,128)}, u32[]{:S(2)}) copy-start(f32[18,5,1,128]{3,1,2,0:T(8,128)} %copy-done.13) | copy-start | bytes 138244
  33.6 3.1 %copy-start.23 = (pred[16,16,128]{2,1,0:T(8,128)(4,1)S(1)}, pred[16,16,128]{2,1,0:T(8,128)(4,1)}, u32[]{:S(2)}) copy-start(pred[16,16,128]{2,1,0:T(8,128)(4,1)} %get-tuple-element.653) | copy-start | bytes 98308
  43.4 4.3 %copy-start.10 = (f32[16,5,16,128]{3,2,1,0:T(8,128)S(1)}, f32[16,5,16,128]{3,2,1,0:T(8,128)}, u32[]{:S(2)}) copy-start(f32[16,5,16,128]{3,2,1,0:T(8,128)} %param.24) | copy-start | bytes 1966084
  91.2 16.6 %all-to-all-start = ((f32[8,1,7680]{2,1,0:T(1,128)}), f32[8,1,7680]{2,1,0:T(1,128)S(1)}, u32[]{:S(2)}, u32[]{:S(2)}) async-start(f32[8,1,7680]{2,1,0:T(1,128)} %reshape.87), calls=%async_computation | async-start | bytes 491520 | tf_op jit(solution)/shard_map/all_to_all | solution.py:92
  117.6 10.8 %all-to-all-start.1 = ((f32[8,5,256]{2,1,0:T(8,128)}), f32[8,5,256]{2,1,0:T(8,128)S(1)}, u32[]{:S(2)}, u32[]{:S(2)}) async-start(f32[8,5,256]{2,1,0:T(8,128)} %get-tuple-element.444), calls=%async_computation.1 | async-start | bytes 131072 | tf_op jit(solution)/shard_map/all_to_all | solution.py:96
  128.5 19.4 %copy-start.19 = (f32[5,5]{1,0:T(8,128)S(1)}, f32[5,5]{1,0:T(8,128)}, u32[]{:S(2)}) copy-start(f32[5,5]{1,0:T(8,128)} %param.33) | copy-start | bytes 304
  189.8 11.5 %all-to-all-start.2 = ((f32[8,1,7680]{2,1,0:T(1,128)}), f32[8,1,7680]{2,1,0:T(1,128)S(1)}, u32[]{:S(2)}, u32[]{:S(2)}) async-start(f32[8,1,7680]{2,1,0:T(1,128)} %reshape.89), calls=%async_computation.2 | async-start | bytes 491520 | tf_op jit(solution)/shard_map/all_to_all | solution.py:101
  211.0 10.2 %all-to-all-start.3 = ((f32[8,5,256]{2,1,0:T(8,128)}), f32[8,5,256]{2,1,0:T(8,128)S(1)}, u32[]{:S(2)}, u32[]{:S(2)}) async-start(f32[8,5,256]{2,1,0:T(8,128)} %get-tuple-element.448), calls=%async_computation.3 | async-start | bytes 131072 | tf_op jit(solution)/shard_map/all_to_all | solution.py:105
  (14 other events, 26.4 us)
where the time goes:
time: 271 us; the launch traced here: 266 us
  other arithmetic  125 us (46%)
  matrix products  42.5 us (16%)
  waiting for transfers between devices  33.3 us (12%)
  starting transfers between devices  32 us (12%)
  local copies, waits for them, and re-layouts  28.1 us (10%)
  loops' own time  3.88 us (1%)
    reduce_sum x64, other arithmetic, volume_operator(): return jnp.sum(blocks * vector[..., None, :, :, :], axis=-3)  61.3 us
    dot_general x72, matrix products, const_apply(): jnp.einsum('ab,...byz->...ayz', matrix, vector, precision=lax.Precision.H...  28.5 us
    unnamed x5, other arithmetic  18.6 us
    dot_general x32, matrix products, couple(): jnp.einsum('ab,bcyz->acyz', matrix, transfer, precision=lax.Precision.HIG...  14.1 us
    dynamic_update_slice x16, other arithmetic, on_device(): final, swept = lax.scan(forward, incoming, (diag_inverse, residual))  12.7 us
    sub x16, other arithmetic, backward(): value - volume_operator(blocks, const_apply(upper_neighbour_block, carry))  12.6 us
    unnamed x68, local copies, waits for them, and re-layouts  11.9 us
    ppermute x3, starting transfers between devices, with_halo(): lax.ppermute(lax.slice_in_dim(block, block.shape[dim] - width, None, axis...  10.3 us
  transfers between devices with their start and end apart: 10, of which 5 were waited for; matrix products, arithmetic and copies ran while one was open for 6% of the time, Pallas kernels for 0%

commit v1 on v0

v1 whole, which is shorter than its diff:
```python
import functools

import jax
import jax.numpy as jnp
from jax import lax
from jax.experimental import pallas as pl
from jax.experimental.pallas import tpu as pltpu
from jax.sharding import PartitionSpec as P

SUB = 8
LANES = 128
MIB = 1 << 20
SHRINK = 2.0**-24
GROW = 2.0**24


def round_up(value, unit):
    return -(-value // unit) * unit


class Sizes:
    def __init__(self, state_shape):
        self.nx, self.comps, self.ny, self.nz = state_shape
        self.parts = lax.axis_size("gx")
        self.vregs = self.ny // SUB
        self.rows = self.ny // self.parts
        assert self.nz == LANES and self.parts % SUB == 0
        assert self.ny % self.parts == 0
        self.square = self.comps * self.comps
        self.map_rows = round_up(3 * self.square * self.rows, SUB)
        self.vec_rows = round_up(2 * self.comps * self.rows, SUB)
        self.edge_count = self.nx * self.comps * self.vregs
        self.edge_rows = SUB * -(-self.edge_count // LANES)

    def start(self, index, vreg, chunk):
        first = vreg * SUB
        return (first % self.parts) * chunk + index * self.rows + first // self.parts


def scatter(sizes, ref, chunk, index, value):
    for vreg in range(sizes.vregs):
        start = sizes.start(index, vreg, chunk)
        ref[pl.ds(start, SUB, stride=chunk), :] = value[vreg * SUB : (vreg + 1) * SUB]


def gather(sizes, ref, chunk, index):
    parts = []
    for vreg in range(sizes.vregs):
        start = sizes.start(index, vreg, chunk)
        parts.append(ref[pl.ds(start, SUB, stride=chunk), :])
    return jnp.concatenate(parts, axis=0)


def combine(terms):
    terms = list(terms)
    while len(terms) > 1:
        terms = [
            terms[i] + terms[i + 1] if i + 1 < len(terms) else terms[i]
            for i in range(0, len(terms), 2)
        ]
    return terms[0]


def maps_kernel(sizes, diag_ref, lower_ref, upper_ref, out_ref, fwd_ref, back_ref, mix_ref):
    comps, nx = sizes.comps, sizes.nx
    span = range(comps)

    def product(x, coupling_ref, negate):
        sign = -1.0 if negate else 1.0
        scale = [[sign * coupling_ref[b, c] for c in span] for b in span]
        rows = []
        for a in span:
            diag = [diag_ref[x, a, b] for b in span]
            rows.append([combine(diag[b] * scale[b][c] for b in span) for c in span])
        return rows

    first = product(0, lower_ref, False)
    for a in span:
        for c in span:
            fwd_ref[0, a, c] = first[a][c] * SHRINK

    def forward(x, carry):
        step = product(x, lower_ref, False)
        for d in span:
            column = [fwd_ref[x - 1, c, d] for c in span]
            for a in span:
                fwd_ref[x, a, d] = combine(step[a][c] * column[c] for c in span)
        return carry

    lax.fori_loop(1, nx, forward, 0)

    last = product(nx - 1, upper_ref, True)
    for a in span:
        for d in span:
            back_ref[(nx - 1) % 2, a, d] = last[a][d]
            mix_ref[(nx - 1) % 2, a, d] = fwd_ref[nx - 1, a, d]

    def backward(count, carry):
        x = nx - 1 - count
        now, before = lax.rem(x, 2), lax.rem(x + 1, 2)
        step = product(x, upper_ref, True)
        for d in span:
            column = [back_ref[before, c, d] for c in span]
            for a in span:
                back_ref[now, a, d] = combine(step[a][c] * column[c] for c in span)
        for d in span:
            column = [mix_ref[before, c, d] for c in span]
            for a in span:
                mix_ref[now, a, d] = fwd_ref[x, a, d] + combine(
                    step[a][c] * column[c] for c in span
                )
        return carry

    lax.fori_loop(1, nx, backward, 0)

    for a in span:
        for d in span:
            index = a * comps + d
            scatter(sizes, out_ref, sizes.map_rows, index, fwd_ref[nx - 1, a, d] * GROW)
            scatter(sizes, out_ref, sizes.map_rows, sizes.square + index, back_ref[0, a, d])
            scatter(sizes, out_ref, sizes.map_rows, 2 * sizes.square + index, mix_ref[0, a, d])


def edges_kernel(sizes, gy_two, gz_two, state_ref, mask_ref, *refs):
    masked_ref, west_ref, east_ref, *rest = refs
    y_refs = rest[: 1 if gy_two else 2]
    z_refs = rest[len(y_refs) :]
    nx, comps = sizes.nx, sizes.comps
    lane = lax.broadcasted_iota(jnp.int32, (SUB, LANES), 1)
    low_z = (lax.axis_index("gz") == 0).astype(jnp.int32)
    shifts = [low_z] if gz_two else [0, 1]
    packed = [[jnp.zeros((SUB, LANES), jnp.float32)] * (sizes.edge_rows // SUB) for _ in shifts]
    low_y = lax.axis_index("gy") == 0
    for x in range(nx):
        fluid = mask_ref[x].astype(jnp.float32)
        for c in range(comps):
            value = state_ref[x, c] * fluid
            masked_ref[x, c] = value
            if x == 0:
                west_ref[c] = value
            if x == nx - 1:
                east_ref[c] = value
            row = pl.ds(x * comps + c, 1)
            bottom, top = value[0:1], value[sizes.ny - 1 : sizes.ny]
            if gy_two:
                y_refs[0][row, :] = jnp.where(low_y, top, bottom)
            else:
                y_refs[0][row, :] = bottom
                y_refs[1][row, :] = top
            for v in range(sizes.vregs):
                index = (x * comps + c) * sizes.vregs + v
                group, place = divmod(index, LANES)
                part = value[v * SUB : (v + 1) * SUB]
                for side, shift in enumerate(shifts):
                    turned = pltpu.roll(part, lax.rem(jnp.int32(place) + shift, LANES), 1)
                    packed[side][group] = jnp.where(lane == place, turned, packed[side][group])
    for side in range(len(shifts)):
        for group, value in enumerate(packed[side]):
            z_refs[side][group * SUB : (group + 1) * SUB, :] = value


def sweep_steps(sizes, diag_ref, lower_ref, upper_ref):
    span = range(sizes.comps)

    def apply(x, vector):
        return [combine(diag_ref[x, a, b] * vector[b] for b in span) for a in span]

    def coupled(matrix_ref, vector):
        return [combine(matrix_ref[a, b] * vector[b] for b in span) for a in span]

    def forward(x, term, carry):
        pushed = coupled(lower_ref, carry)
        return apply(x, [term[a] + pushed[a] for a in span])

    def backward(x, value, carry):
        pulled = apply(x, coupled(upper_ref, carry))
        return [value[a] - pulled[a] for a in span]

    return forward, backward


def residual_kernel(
    sizes, gy_two, gz_two,
    state_ref, masked_ref, source_ref, mask_ref, kind_ref, side_ref,
    center_ref, flux_ref, wall_ref, diag_ref, lower_ref, upper_ref,
    west_ref, east_ref, south_ref, north_ref, below_ref, above_ref,
    residual_ref, out_ref, swept_ref, zlow_ref, zhigh_ref,
):
    nx, comps, ny = sizes.nx, sizes.comps, sizes.ny
    span = range(comps)
    shape = (ny, LANES)
    lane = lax.broadcasted_iota(jnp.int32, (SUB, LANES), 1)
    row_index = lax.broadcasted_iota(jnp.int32, shape, 0)
    full_lane = lax.broadcasted_iota(jnp.int32, shape, 1)
    low_y = lax.axis_index("gy") == 0
    low_z = lax.axis_index("gz") == 0
    below, above = below_ref[...], above_ref[...]
    if gz_two:
        below = jnp.where(low_z, 0.0, below)
        above = jnp.where(low_z, above, 0.0)
    zlow_ref[...] = below
    zhigh_ref[...] = above
    forward, backward = sweep_steps(sizes, diag_ref, lower_ref, upper_ref)

    def edge_column(ref, x, c, target):
        parts = []
        for v in range(sizes.vregs):
            index = (x * comps + c) * sizes.vregs + v
            group = pl.multiple_of((index // LANES) * SUB, SUB)
            shift = lax.rem(target + LANES - lax.rem(index, LANES), LANES)
            parts.append(pltpu.roll(ref[pl.ds(group, SUB), :], shift, 1))
        return jnp.concatenate(parts, axis=0)

    def plane(x, carry):
        side = side_ref[x]
        fluid = mask_ref[x].astype(jnp.float32)
        kind = kind_ref[x]
        weight = fluid * jnp.where(kind == 0, 1.0, jnp.where(kind == 1, 2.0, 4.0))
        walled = side < 6
        open_face = [side != d for d in range(6)]
        total = [None] * comps

        def add(get, c, value):
            for a in span:
                term = get(a, c) * value
                total[a] = term if total[a] is None else total[a] + term

        for c in span:
            value = state_ref[x, c]
            add(lambda a, b: center_ref[a, b], c, value)
            add(lambda a, b: wall_ref[a, b], c, jnp.where(walled, value, 0.0))
            masked = masked_ref[x, c]
            row = pl.ds(x * comps + c, 1)
            south = jnp.broadcast_to(south_ref[row, :], shape)
            north = jnp.broadcast_to(north_ref[row, :], shape)
            if gy_two:
                south = jnp.where(low_y, 0.0, south)
                north = jnp.where(low_y, north, 0.0)
            neighbours = [
                jnp.where(x == 0, west_ref[c], masked_ref[jnp.maximum(x - 1, 0), c]),
                jnp.where(x == nx - 1, east_ref[c], masked_ref[jnp.minimum(x + 1, nx - 1), c]),
                jnp.where(row_index == 0, south, pltpu.roll(masked, 1, 0)),
                jnp.where(row_index == ny - 1, north, pltpu.roll(masked, ny - 1, 0)),
                jnp.where(full_lane == 0, edge_column(zlow_ref, x, c, 0), pltpu.roll(masked, 1, 1)),
                jnp.where(
                    full_lane == LANES - 1,
                    edge_column(zhigh_ref, x, c, LANES - 1),
                    pltpu.roll(masked, LANES - 1, 1),
                ),
            ]
            for d in range(6):
                add(
                    functools.partial(lambda e, a, b: flux_ref[e, a, b], d),
                    c,
                    jnp.where(open_face[d], neighbours[d], 0.0),
                )
        term = [weight * (source_ref[x, a] - total[a]) for a in span]
        for a in span:
            residual_ref[x, a] = term[a]
        carry = forward(x, term, carry)
        for a in span:
            swept_ref[x, a] = carry[a]
        return tuple(carry)

    zeroed = tuple(jnp.zeros(shape, jnp.float32) for _ in span)
    carry = lax.fori_loop(0, nx, plane, zeroed)
    for a in span:
        scatter(sizes, out_ref, sizes.vec_rows, a, carry[a])

    def back(count, carry):
        x = nx - 1 - count
        return tuple(backward(x, [swept_ref[x, a] for a in span], carry))

    carry = lax.fori_loop(0, nx, back, zeroed)
    for a in span:
        scatter(sizes, out_ref, sizes.vec_rows, comps + a, carry[a])


def chain_kernel(sizes, maps_ref, vec_ref, out_ref):
    comps, rows, square = sizes.comps, sizes.rows, sizes.square
    span = range(comps)

    def item(ref, chunk, part, index):
        return ref[pl.ds(part * chunk + index * rows, rows), :]

    def matrix(part, base, vector):
        return [
            combine(
                item(maps_ref, sizes.map_rows, part, base + a * comps + b) * vector[b]
                for b in span
            )
            for a in span
        ]

    carry = [jnp.zeros((rows, LANES), jnp.float32)] * comps
    incoming = []
    for part in range(sizes.parts):
        incoming.append(carry)
        for a in span:
            out_ref[pl.ds(part * sizes.vec_rows + a * rows, rows), :] = carry[a]
        moved = matrix(part, 0, carry)
        carry = [moved[a] + item(vec_ref, sizes.vec_rows, part, a) for a in span]
    carry = [jnp.zeros((rows, LANES), jnp.float32)] * comps
    for part in reversed(range(sizes.parts)):
        for a in span:
            out_ref[pl.ds(part * sizes.vec_rows + (comps + a) * rows, rows), :] = carry[a]
        moved = matrix(part, square, carry)
        mixed = matrix(part, 2 * square, incoming[part])
        carry = [
            moved[a] + (mixed[a] * GROW + item(vec_ref, sizes.vec_rows, part, comps + a))
            for a in span
        ]


def finish_kernel(sizes, residual_ref, diag_ref, lower_ref, upper_ref, vec_ref, update_ref, swept_ref):
    comps, nx = sizes.comps, sizes.nx
    span = range(comps)
    forward, backward = sweep_steps(sizes, diag_ref, lower_ref, upper_ref)
    carry = tuple(gather(sizes, vec_ref, sizes.vec_rows, a) for a in span)

    def ahead(x, carry):
        carry = forward(x, [residual_ref[x, a] for a in span], carry)
        for a in span:
            swept_ref[x, a] = carry[a]
        return tuple(carry)

    lax.fori_loop(0, nx, ahead, carry)
    carry = tuple(gather(sizes, vec_ref, sizes.vec_rows, comps + a) for a in span)

    def back(count, carry):
        x = nx - 1 - count
        carry = backward(x, [swept_ref[x, a] for a in span], carry)
        for a in span:
            update_ref[x, a] = carry[a]
        return tuple(carry)

    lax.fori_loop(0, nx, back, carry)


VMEM = pl.BlockSpec(memory_space=pltpu.VMEM)
SMEM = pl.BlockSpec(memory_space=pltpu.SMEM)


def call(kernel, name, in_specs, outs, scratch, limit, flops):
    return pl.pallas_call(
        kernel,
        name=name,
        in_specs=in_specs,
        out_specs=tuple(VMEM for _ in outs),
        out_shape=tuple(jax.ShapeDtypeStruct(shape, jnp.float32) for shape in outs),
        scratch_shapes=[pltpu.VMEM(shape, jnp.float32) for shape in scratch],
        compiler_params=pltpu.CompilerParams(vmem_limit_bytes=limit * MIB),
        cost_estimate=pl.CostEstimate(flops=flops, bytes_accessed=1 << 20, transcendentals=0),
    )


def shifted(low, high, axis, count):
    if count == 2:
        other = lax.ppermute(low, axis, [(0, 1), (1, 0)])
        return other, other
    up = [(i, i + 1) for i in range(count - 1)]
    down = [(target, origin) for origin, target in up]
    return lax.ppermute(high, axis, up), lax.ppermute(low, axis, down)


def spread(sizes, array, chunk):
    blocks = array.reshape(sizes.parts, chunk, LANES)
    moved = lax.all_to_all(blocks, "gx", split_axis=0, concat_axis=0, tiled=True)
    return moved.reshape(array.shape)


def on_device(
    state_field, source, fluid_mask, cell_kind, boundary_side_number,
    center_matrix, flux_jacobian_blocks, wall_matrix,
    diag_inverse, lower_coupling, upper_neighbour_block,
):
    sizes = Sizes(state_field.shape)
    nx, comps, ny, nz = state_field.shape
    parts = sizes.parts
    gy, gz = lax.axis_size("gy"), lax.axis_size("gz")
    gy_two, gz_two = gy == 2, gz == 2
    square = (nx, comps, comps, ny, nz)
    face = (comps, ny, nz)
    cells = nx * ny * nz

    (maps,) = call(
        functools.partial(maps_kernel, sizes), "maps", [VMEM, SMEM, SMEM],
        [(parts * sizes.map_rows, LANES)],
        [square, (2,) + square[1:], (2,) + square[1:]],
        12, 1150 * cells,
    )(diag_inverse, lower_coupling, upper_neighbour_block)

    y_count, z_count = (1 if gy_two else 2), (1 if gz_two else 2)
    masked, west, east, *rest = call(
        functools.partial(edges_kernel, sizes, gy_two, gz_two), "edges", [VMEM, VMEM],
        [state_field.shape, face, face]
        + [(nx * comps, nz)] * y_count + [(sizes.edge_rows, LANES)] * z_count,
        [], 8, 10 * cells,
    )(state_field, fluid_mask)
    y_low, y_high = rest[0], rest[y_count - 1]
    z_low, z_high = rest[y_count], rest[y_count + z_count - 1]

    from_west, from_east = shifted(west, east, "gx", parts)
    from_south, from_north = shifted(y_low, y_high, "gy", gy)
    from_below, from_above = shifted(z_low, z_high, "gz", gz)
    maps = spread(sizes, maps, sizes.map_rows)

    residual, vectors = call(
        functools.partial(residual_kernel, sizes, gy_two, gz_two), "residual",
        [VMEM] * 6 + [SMEM] * 3 + [VMEM] + [SMEM] * 2 + [VMEM] * 6,
        [state_field.shape, (parts * sizes.vec_rows, LANES)],
        [state_field.shape, (sizes.edge_rows, LANES), (sizes.edge_rows, LANES)],
        16, 650 * cells,
    )(
        state_field, masked, source, fluid_mask, cell_kind, boundary_side_number,
        center_matrix, flux_jacobian_blocks, wall_matrix,
        diag_inverse, lower_coupling, upper_neighbour_block,
        from_west, from_east, from_south, from_north, from_below, from_above,
    )
    vectors = spread(sizes, vectors, sizes.vec_rows)
    (incoming,) = call(
        functools.partial(chain_kernel, sizes), "chain", [VMEM, VMEM],
        [(parts * sizes.vec_rows, LANES)], [], 4, 1200 * ny * nz,
    )(maps, vectors)
    incoming = spread(sizes, incoming, sizes.vec_rows)
    (update,) = call(
        functools.partial(finish_kernel, sizes), "finish", [VMEM, VMEM, SMEM, SMEM, VMEM],
        [state_field.shape], [state_field.shape], 8, 200 * cells,
    )(residual, diag_inverse, lower_coupling, upper_neighbour_block, incoming)
    return update, residual


def solution(mesh):
    cells = P("gx", None, "gy", "gz")
    flags = P("gx", "gy", "gz")
    in_specs = (
        cells, cells, flags, flags, flags, P(), P(), P(),
        P("gx", None, None, "gy", "gz"), P(), P(),
    )
    return jax.shard_map(
        on_device, mesh=mesh, in_specs=in_specs, out_specs=(cells, cells), check_vma=False
    )
```

time: 271 us -> 80.9 us (0.30); the launches traced: 266 us -> 80.1 us
  other arithmetic: 125 us -> 0 us
  matrix products: 42.5 us -> 0 us
  blocking collectives: 0 us -> 31.6 us
  waiting for transfers between devices: 33.3 us -> 2.28 us
  starting transfers between devices: 32 us -> 14.2 us
  Pallas kernels: 0 us -> 17.1 us
  local copies, waits for them, and re-layouts: 28.1 us -> 14.2 us
  loops' own time: 3.88 us -> 0 us
    reduce_sum x112 -> x0, other arithmetic: 64.3 us -> none  [the longest x64 61.3 us: volume_operator(): return jnp.sum(blocks * vector[..., None, :, :, :], axis=-3)]
    dot_general x104 -> x0, matrix products: 42.5 us -> none  [the longest x72 28.5 us: const_apply(): jnp.einsum('ab,...byz->...ayz', matrix, vector, precision=lax.Precision.H...]
    all_to_all x0 -> x2, blocking collectives: none -> 31.6 us  [spread(): lax.all_to_all(blocks, 'gx', split_axis=0, concat_axis=0, tiled=True)]
    all_to_all x4 -> x1, waiting for transfers between devices: 30.5 us -> 0.01 us  [spread(): lax.all_to_all(blocks, 'gx', split_axis=0, concat_axis=0, tiled=True)]
    dynamic_update_slice x32 -> x0, other arithmetic: 22.3 us -> none  [the longest x16 12.7 us: on_device(): final, swept = lax.scan(forward, incoming, (diag_inverse, residual))]
    unnamed x5 -> x0, other arithmetic: 18.6 us -> none
    pallas_call x0 -> x5, Pallas kernels: none -> 17.1 us  [the longest x1 7.17 us: on_device(): call(functools.partial(residual_kernel, sizes, gy_two, gz_two), 'residual...]
    sub x32 -> x0, other arithmetic: 12.8 us -> none  [the longest x16 12.6 us: backward(): value - volume_operator(blocks, const_apply(upper_neighbour_block, carry))]
  transfers between devices with their start and end apart: 10 -> 5, of which waited for: 5 -> 2; matrix products, arithmetic and copies ran while one was open for 6% -> 1% of each run, Pallas kernels for 0% -> 9%
where the time goes in v1:
time: 80.9 us; the launch traced here: 80.1 us
  blocking collectives  31.6 us (39%)
  Pallas kernels  17.1 us (21%)
  local copies, waits for them, and re-layouts  14.2 us (18%)
  starting transfers between devices  14.2 us (18%)
  waiting for transfers between devices  2.28 us (3%)
    all_to_all x2, blocking collectives, spread(): lax.all_to_all(blocks, 'gx', split_axis=0, concat_axis=0, tiled=True)  31.6 us
    unnamed x35, local copies, waits for them, and re-layouts  14.2 us
    pallas_call x1, Pallas kernels, on_device(): call(functools.partial(residual_kernel, sizes, gy_two, gz_two), 'residual...  7.17 us
    pallas_call x1, Pallas kernels, on_device(): call(functools.partial(maps_kernel, sizes), 'maps', [VMEM, SMEM, SMEM], [...  6.86 us
    all_to_all x1, starting transfers between devices, spread(): lax.all_to_all(blocks, 'gx', split_axis=0, concat_axis=0, tiled=True)  6.42 us
    ppermute x2, starting transfers between devices, shifted(): return (lax.ppermute(high, axis, up), lax.ppermute(low, axis, down))  6.17 us
    pallas_call x1, Pallas kernels, on_device(): call(functools.partial(finish_kernel, sizes), 'finish', [VMEM, VMEM, SMEM...  2.65 us
    ppermute x2, waiting for transfers between devices, shifted(): return (lax.ppermute(high, axis, up), lax.ppermute(low, axis, down))  1.84 us
  transfers between devices with their start and end apart: 5, of which 2 were waited for; matrix products, arithmetic and copies ran while one was open for 1% of the time, Pallas kernels for 9%

profile of v1, /device:TPU:0, one launch (start us, length us, event | category | flops | bytes accessed | tf_op | source)
XLA Modules:
  0.0 80.1 jit_solution(4086043078485819059)
XLA Ops:
  0.6 1.1 %copy-done.2 = f32[16,5,16,128]{3,2,1,0:T(8,128)S(1)} copy-done((f32[16,5,16,128]{3,2,1,0:T(8,128)S(1)}, f32[16,5,16,128]{3,2,1,0:T(8,128)}, u32[]{:S(2)}) %copy-start.2) | copy-done | bytes 655384
  1.7 0.9 %copy-done.7 = s32[16,16,128]{2,1,0:T(8,128)S(1)} copy-done((s32[16,16,128]{2,1,0:T(8,128)S(1)}, s32[16,16,128]{2,1,0:T(8,128)}, u32[]{:S(2)}) %copy-start.7) | copy-done | bytes 131096
  2.9 4.9 %collective-permute-start = (f32[5,16,128]{2,1,0:T(8,128)S(1)}, f32[5,16,128]{2,1,0:T(8,128)S(1)}, u32[]{:S(2)}, u32[]{:S(2)}) collective-permute-start(f32[5,16,128]{2,1,0:T(8,128)S(1)} %get-tuple-element.10), channel_id=1, source_target_pairs={{0,4},{4,8},{8,12},{12,16},{16,20},{20,24},{24,28},{1,5},{5,9},{9,... | collective-permute-start | bytes 122888 | tf_op jit(solution)/shard_map/ppermute | solution.py:363
  7.8 1.3 %collective-permute-start.1 = (f32[5,16,128]{2,1,0:T(8,128)S(1)}, f32[5,16,128]{2,1,0:T(8,128)S(1)}, u32[]{:S(2)}, u32[]{:S(2)}) collective-permute-start(f32[5,16,128]{2,1,0:T(8,128)S(1)} %get-tuple-element.11), channel_id=1, source_target_pairs={{4,0},{8,4},{12,8},{16,12},{20,16},{24,20},{28,24},{5,1},{9,5},{13... | collective-permute-start | bytes 122888 | tf_op jit(solution)/shard_map/ppermute | solution.py:363
  9.1 1.6 %collective-permute-start.2 = (f32[80,128]{1,0:T(8,128)S(1)}, f32[80,128]{1,0:T(8,128)S(1)}, u32[]{:S(2)}, u32[]{:S(2)}) collective-permute-start(f32[80,128]{1,0:T(8,128)S(1)} %get-tuple-element.12), channel_id=1, source_target_pairs={{0,2},{2,0},{1,3},{3,1},{4,6},{6,4},{5,7},{7,5},{8,10},{10,8},{9,1... | collective-permute-start | bytes 122888 | tf_op jit(solution)/shard_map/ppermute | solution.py:359
  10.7 0.7 copy.13.flux_ref
  11.9 1.8 %collective-permute-done.1.east_ref = f32[5,16,128]{2,1,0:T(8,128)S(1)} collective-permute-done((f32[5,16,128]{2,1,0:T(8,128)S(1)}, f32[5,16,128]{2,1,0:T(8,128)S(1)}, u32[]{:S(2)}, u32[]{:S(2)}) %collective-permute-start.1) | collective-permute-done | bytes 40992 | tf_op jit(solution)/shard_map/ppermute | solution.py:363
  13.7 1.9 %copy-done = f32[16,5,5,16,128]{4,3,2,1,0:T(8,128)S(1)} copy-done((f32[16,5,5,16,128]{4,3,2,1,0:T(8,128)S(1)}, f32[16,5,5,16,128]{4,3,2,1,0:T(8,128)}, u32[]{:S(2)}) %copy-start) | copy-done | bytes 3276824
  15.6 1.1 %copy-done.3 = f32[16,5,16,128]{3,2,1,0:T(8,128)S(1)} copy-done((f32[16,5,16,128]{3,2,1,0:T(8,128)S(1)}, f32[16,5,16,128]{3,2,1,0:T(8,128)}, u32[]{:S(2)}) %copy-start.3) | copy-done | bytes 655384
  16.7 1.1 %copy-done.6 = f32[16,5,16,128]{3,2,1,0:T(8,128)S(1)} copy-done((f32[16,5,16,128]{3,2,1,0:T(8,128)S(1)}, f32[16,5,16,128]{3,2,1,0:T(8,128)}, u32[]{:S(2)}) %copy-start.6) | copy-done | bytes 655384
  17.8 0.9 %copy-done.8 = s32[16,16,128]{2,1,0:T(8,128)S(1)} copy-done((s32[16,16,128]{2,1,0:T(8,128)S(1)}, s32[16,16,128]{2,1,0:T(8,128)}, u32[]{:S(2)}) %copy-start.8) | copy-done | bytes 131096
  18.7 0.9 %copy-done.9 = s32[16,16,128]{2,1,0:T(8,128)S(1)} copy-done((s32[16,16,128]{2,1,0:T(8,128)S(1)}, s32[16,16,128]{2,1,0:T(8,128)}, u32[]{:S(2)}) %copy-start.9) | copy-done | bytes 131096
  19.6 0.9 %copy-done.10 = s32[16,16,128]{2,1,0:T(8,128)S(1)} copy-done((s32[16,16,128]{2,1,0:T(8,128)S(1)}, s32[16,16,128]{2,1,0:T(8,128)}, u32[]{:S(2)}) %copy-start.10) | copy-done | bytes 131096
  20.5 0.7 copy-done.11
  21.2 0.7 copy-done.13
  21.9 0.7 copy-done.15
  23.3 7.2 %residual.1 = (f32[16,5,16,128]{3,2,1,0:T(8,128)}, f32[192,128]{1,0:T(8,128)}) custom-call(f32[16,5,16,128]{3,2,1,0:T(8,128)S(1)} %copy-done.3, f32[16,5,16,128]{3,2,1,0:T(8,128)S(1)} %get-tuple-element.9.masked_ref, f32[16,5,16,128]{3,2,1,0:T(8,128)S(1)} %copy-done.6, s32[16,16,128]{2,1,0:T(8,128)S(1)} %copy-done.8, s32[16,16,128]{2,1,0:T(8,128)S(1)} %copy-done.9, ...), custom_call_target="tpu_custom_call" | custom-call | flops 21299200 | bytes 1048576 | tf_op jit(solution)/shard_map/residual/pallas_call | solution.py:408
  30.4 6.4 %all-to-all-start.1 = ((f32[8,24,128]{2,1,0:T(8,128)}), f32[8,24,128]{2,1,0:T(8,128)S(1)}, u32[]{:S(2)}, u32[]{:S(2)}) async-start(f32[8,24,128]{2,1,0:T(8,128)} %bitcast.2), calls=%async_computation.1 | async-start | bytes 196608 | tf_op jit(solution)/shard_map/all_to_all | solution.py:368
  36.9 6.9 %maps.1 = f32[1216,128]{1,0:T(8,128)S(1)} custom-call(f32[16,5,5,16,128]{4,3,2,1,0:T(8,128)S(1)} %copy-done.1, f32[5,5]{1,0:T(8,128)S(1)} %copy-done.12, f32[5,5]{1,0:T(8,128)S(1)} %copy-done.14), custom_call_target="tpu_custom_call" | custom-call | flops 37683200 | bytes 1048576 | tf_op jit(solution)/shard_map/maps/pallas_call | solution.py:386
  43.8 0.8 %copy-done.4 = f32[1216,128]{1,0:T(8,128)} copy-done((f32[1216,128]{1,0:T(8,128)}, f32[1216,128]{1,0:T(8,128)S(1)}, u32[]{:S(2)}) %copy-start.4) | copy-done | bytes 622616
  44.6 21.6 %all_to_all.15 = f32[8,152,128]{2,1,0:T(8,128)S(1)} all-to-all(f32[8,152,128]{2,1,0:T(8,128)} %bitcast.7), channel_id=1, replica_groups=mesh['gx'=8,'gy'=2,'gz'=2] {'gx'}, dimensions={0} | all-to-all | bytes 1245184 | tf_op jit(solution)/shard_map/all_to_all | solution.py:368
  66.3 10.1 %all_to_all.16 = f32[8,24,128]{2,1,0:T(8,128)S(1)} all-to-all(f32[8,24,128]{2,1,0:T(8,128)S(1)} %bitcast.9), channel_id=1, replica_groups=mesh['gx'=8,'gy'=2,'gz'=2] {'gx'}, dimensions={0} | all-to-all | bytes 196608 | tf_op jit(solution)/shard_map/all_to_all | solution.py:368
  76.4 1.1 %copy-done.5 = f32[16,5,16,128]{3,2,1,0:T(8,128)S(1)} copy-done((f32[16,5,16,128]{3,2,1,0:T(8,128)S(1)}, f32[16,5,16,128]{3,2,1,0:T(8,128)}, u32[]{:S(2)}) %copy-start.5) | copy-done | bytes 655384
  77.4 2.6 %finish.1 = f32[16,5,16,128]{3,2,1,0:T(8,128)} custom-call(f32[16,5,16,128]{3,2,1,0:T(8,128)S(1)} %copy-done.5, f32[16,5,5,16,128]{4,3,2,1,0:T(8,128)S(1)} %copy-done.1, f32[5,5]{1,0:T(8,128)S(1)} %copy-done.12, f32[5,5]{1,0:T(8,128)S(1)} %copy-done.14, f32[192,128]{1,0:T(8,128)S(1)} %bitcast.10), custom_call_target="tpu_custom_call" | custom-call | flops 6553600 | bytes 1048576 | tf_op jit(solution)/shard_map/finish/pallas_call | solution.py:426
  (28 shorter events, 1.6 us)
Async XLA Ops:
  0.6 1.1 %copy-start.2 = (f32[16,5,16,128]{3,2,1,0:T(8,128)S(1)}, f32[16,5,16,128]{3,2,1,0:T(8,128)}, u32[]{:S(2)}) copy-start(f32[16,5,16,128]{3,2,1,0:T(8,128)} %state_ref.3) | copy-start | bytes 1966084
  1.7 0.9 %copy-start.7 = (s32[16,16,128]{2,1,0:T(8,128)S(1)}, s32[16,16,128]{2,1,0:T(8,128)}, u32[]{:S(2)}) copy-start(s32[16,16,128]{2,1,0:T(8,128)} %mask_ref.3) | copy-start | bytes 393220
  2.6 34.2 %copy-start.12 = (f32[5,5]{1,0:T(8,128)S(1)}, f32[5,5]{1,0:T(8,128)}, u32[]{:S(2)}) copy-start(f32[5,5]{1,0:T(8,128)} %lower_ref.5) | copy-start | bytes 304
  2.6 34.2 %copy-start.14 = (f32[5,5]{1,0:T(8,128)S(1)}, f32[5,5]{1,0:T(8,128)}, u32[]{:S(2)}) copy-start(f32[5,5]{1,0:T(8,128)} %upper_ref.5) | copy-start | bytes 304
  2.9 8.9 %collective-permute-start = (f32[5,16,128]{2,1,0:T(8,128)S(1)}, f32[5,16,128]{2,1,0:T(8,128)S(1)}, u32[]{:S(2)}, u32[]{:S(2)}) collective-permute-start(f32[5,16,128]{2,1,0:T(8,128)S(1)} %get-tuple-element.10), channel_id=1, source_target_pairs={{0,4},{4,8},{8,12},{12,16},{16,20},{20,24},{24,28},{1,5},{5,9},{9,... | collective-permute-start | bytes 122888 | tf_op jit(solution)/shard_map/ppermute | solution.py:363
  7.8 5.9 %collective-permute-start.1 = (f32[5,16,128]{2,1,0:T(8,128)S(1)}, f32[5,16,128]{2,1,0:T(8,128)S(1)}, u32[]{:S(2)}, u32[]{:S(2)}) collective-permute-start(f32[5,16,128]{2,1,0:T(8,128)S(1)} %get-tuple-element.11), channel_id=1, source_target_pairs={{4,0},{8,4},{12,8},{16,12},{20,16},{24,20},{28,24},{5,1},{9,5},{13... | collective-permute-start | bytes 122888 | tf_op jit(solution)/shard_map/ppermute | solution.py:363
  9.1 4.6 %collective-permute-start.2 = (f32[80,128]{1,0:T(8,128)S(1)}, f32[80,128]{1,0:T(8,128)S(1)}, u32[]{:S(2)}, u32[]{:S(2)}) collective-permute-start(f32[80,128]{1,0:T(8,128)S(1)} %get-tuple-element.12), channel_id=1, source_target_pairs={{0,2},{2,0},{1,3},{3,1},{4,6},{6,4},{5,7},{7,5},{8,10},{10,8},{9,1... | collective-permute-start | bytes 122888 | tf_op jit(solution)/shard_map/ppermute | solution.py:359
  10.7 1.2 %collective-permute-start.3 = (f32[16,128]{1,0:T(8,128)S(1)}, f32[16,128]{1,0:T(8,128)S(1)}, u32[]{:S(2)}, u32[]{:S(2)}) collective-permute-start(f32[16,128]{1,0:T(8,128)S(1)} %get-tuple-element.13), channel_id=1, source_target_pairs={{0,1},{1,0},{2,3},{3,2},{4,5},{5,4},{6,7},{7,6},{8,9},{9,8},{10,11... | collective-permute-start | bytes 24584 | tf_op jit(solution)/shard_map/ppermute | solution.py:359
  13.7 1.9 %copy-start = (f32[16,5,5,16,128]{4,3,2,1,0:T(8,128)S(1)}, f32[16,5,5,16,128]{4,3,2,1,0:T(8,128)}, u32[]{:S(2)}) copy-start(f32[16,5,5,16,128]{4,3,2,1,0:T(8,128)} %diag_ref.5) | copy-start | bytes 9830404
  15.6 1.1 %copy-start.3 = (f32[16,5,16,128]{3,2,1,0:T(8,128)S(1)}, f32[16,5,16,128]{3,2,1,0:T(8,128)}, u32[]{:S(2)}) copy-start(f32[16,5,16,128]{3,2,1,0:T(8,128)} %state_ref.3) | copy-start | bytes 1966084
  16.7 1.1 %copy-start.6 = (f32[16,5,16,128]{3,2,1,0:T(8,128)S(1)}, f32[16,5,16,128]{3,2,1,0:T(8,128)}, u32[]{:S(2)}) copy-start(f32[16,5,16,128]{3,2,1,0:T(8,128)} %source_ref.1) | copy-start | bytes 1966084
  17.8 0.9 %copy-start.8 = (s32[16,16,128]{2,1,0:T(8,128)S(1)}, s32[16,16,128]{2,1,0:T(8,128)}, u32[]{:S(2)}) copy-start(s32[16,16,128]{2,1,0:T(8,128)} %mask_ref.3) | copy-start | bytes 393220
  18.7 0.9 %copy-start.9 = (s32[16,16,128]{2,1,0:T(8,128)S(1)}, s32[16,16,128]{2,1,0:T(8,128)}, u32[]{:S(2)}) copy-start(s32[16,16,128]{2,1,0:T(8,128)} %kind_ref.1) | copy-start | bytes 393220
  19.6 0.9 %copy-start.10 = (s32[16,16,128]{2,1,0:T(8,128)S(1)}, s32[16,16,128]{2,1,0:T(8,128)}, u32[]{:S(2)}) copy-start(s32[16,16,128]{2,1,0:T(8,128)} %side_ref.1) | copy-start | bytes 393220
  20.5 0.7 copy-start.11
  21.2 0.7 copy-start.13
  21.9 0.7 copy-start.15
  22.6 0.7 copy-start.16
  23.3 13.6 %copy-start.1 = (f32[16,5,5,16,128]{4,3,2,1,0:T(8,128)S(1)}, f32[16,5,5,16,128]{4,3,2,1,0:T(8,128)}, u32[]{:S(2)}) copy-start(f32[16,5,5,16,128]{4,3,2,1,0:T(8,128)} %diag_ref.5) | copy-start | bytes 9830404
  30.4 14.1 %all-to-all-start.1 = ((f32[8,24,128]{2,1,0:T(8,128)}), f32[8,24,128]{2,1,0:T(8,128)S(1)}, u32[]{:S(2)}, u32[]{:S(2)}) async-start(f32[8,24,128]{2,1,0:T(8,128)} %bitcast.2), calls=%async_computation.1 | async-start | bytes 196608 | tf_op jit(solution)/shard_map/all_to_all | solution.py:368
  43.7 0.8 %copy-start.4 = (f32[1216,128]{1,0:T(8,128)}, f32[1216,128]{1,0:T(8,128)S(1)}, u32[]{:S(2)}) copy-start(f32[1216,128]{1,0:T(8,128)S(1)} %maps.1) | copy-start | bytes 1867780
  76.4 1.1 %copy-start.5 = (f32[16,5,16,128]{3,2,1,0:T(8,128)S(1)}, f32[16,5,16,128]{3,2,1,0:T(8,128)}, u32[]{:S(2)}) copy-start(f32[16,5,16,128]{3,2,1,0:T(8,128)} %get-tuple-element.8.residual_ref) | copy-start | bytes 1966084

commit v2 on v1

--- a/solution.py
+++ b/solution.py
@@ -27,7 +27,7 @@
         assert self.nz == LANES and self.parts % SUB == 0
         assert self.ny % self.parts == 0
         self.square = self.comps * self.comps
-        self.map_rows = round_up(3 * self.square * self.rows, SUB)
+        self.map_rows = round_up((3 * self.square + 2 * self.comps) * self.rows, SUB)
         self.vec_rows = round_up(2 * self.comps * self.rows, SUB)
         self.edge_count = self.nx * self.comps * self.vregs
         self.edge_rows = SUB * -(-self.edge_count // LANES)
@@ -49,6 +49,9 @@
         start = sizes.start(index, vreg, chunk)
         parts.append(ref[pl.ds(start, SUB, stride=chunk), :])
     return jnp.concatenate(parts, axis=0)
+
+
+MOVED = ("state", "source", "mask", "kind", "side", "center", "flux", "wall", "lower", "upper")
 
 
 def combine(terms):
@@ -61,9 +64,35 @@
     return terms[0]
 
 
-def maps_kernel(sizes, diag_ref, lower_ref, upper_ref, out_ref, fwd_ref, back_ref, mix_ref):
+def maps_kernel(
+    sizes, diag_hbm, *refs,
+):
+    count = len(MOVED)
+    sources, out_ref, diag_ref = refs[:count], refs[count], refs[count + 1]
+    targets = refs[count + 2 : 2 * count + 2]
+    fwd_ref, back_ref, mix_ref, lower_ref, upper_ref, plane_sems, sems, scalar_sems = refs[2 * count + 2 :]
     comps, nx = sizes.comps, sizes.nx
     span = range(comps)
+    scalars = [
+        pltpu.make_async_copy(sources[MOVED.index(name)], ref, scalar_sems.at[i])
+        for i, (name, ref) in enumerate((("lower", lower_ref), ("upper", upper_ref)))
+    ]
+    for copy in scalars:
+        copy.start()
+
+    def plane_copy(x):
+        return pltpu.make_async_copy(diag_hbm.at[x], diag_ref.at[x], plane_sems.at[x])
+
+    for x in range(nx):
+        plane_copy(x).start()
+    moves = [
+        pltpu.make_async_copy(source, target, sems.at[i])
+        for i, (source, target) in enumerate(zip(sources, targets))
+    ]
+    for copy in moves:
+        copy.start()
+    for copy in scalars:
+        copy.wait()
 
     def product(x, coupling_ref, negate):
         sign = -1.0 if negate else 1.0
@@ -74,12 +103,14 @@
             rows.append([combine(diag[b] * scale[b][c] for b in span) for c in span])
         return rows
 
+    plane_copy(0).wait()
     first = product(0, lower_ref, False)
     for a in span:
         for c in span:
             fwd_ref[0, a, c] = first[a][c] * SHRINK
 
     def forward(x, carry):
+        plane_copy(x).wait()
         step = product(x, lower_ref, False)
         for d in span:
             column = [fwd_ref[x - 1, c, d] for c in span]
@@ -119,6 +150,8 @@
             scatter(sizes, out_ref, sizes.map_rows, index, fwd_ref[nx - 1, a, d] * GROW)
             scatter(sizes, out_ref, sizes.map_rows, sizes.square + index, back_ref[0, a, d])
             scatter(sizes, out_ref, sizes.map_rows, 2 * sizes.square + index, mix_ref[0, a, d])
+    for copy in moves:
+        copy.wait()
 
 
 def edges_kernel(sizes, gy_two, gz_two, state_ref, mask_ref, *refs):
@@ -183,8 +216,8 @@
     sizes, gy_two, gz_two,
     state_ref, masked_ref, source_ref, mask_ref, kind_ref, side_ref,
     center_ref, flux_ref, wall_ref, diag_ref, lower_ref, upper_ref,
-    west_ref, east_ref, south_ref, north_ref, below_ref, above_ref,
-    residual_ref, out_ref, swept_ref, zlow_ref, zhigh_ref,
+    west_ref, east_ref, south_ref, north_ref, below_ref, above_ref, maps_ref,
+    residual_hbm, term_ref, out_ref, swept_ref, zlow_ref, zhigh_ref, sems,
 ):
     nx, comps, ny = sizes.nx, sizes.comps, sizes.ny
     span = range(comps)
@@ -211,7 +244,14 @@
             parts.append(pltpu.roll(ref[pl.ds(group, SUB), :], shift, 1))
         return jnp.concatenate(parts, axis=0)
 
+    def leave(x):
+        return pltpu.make_async_copy(term_ref.at[x], residual_hbm.at[x], sems.at[x])
+
     def plane(x, carry):
+        @pl.when(x > 0)
+        def send():
+            leave(x - 1).start()
+
         side = side_ref[x]
         fluid = mask_ref[x].astype(jnp.float32)
         kind = kind_ref[x]
@@ -250,13 +290,13 @@
             ]
             for d in range(6):
                 add(
-                    functools.partial(lambda e, a, b: flux_ref[e, a, b], d),
+                    functools.partial(lambda e, a, b: flux_ref[a, e, b], d),
                     c,
                     jnp.where(open_face[d], neighbours[d], 0.0),
                 )
         term = [weight * (source_ref[x, a] - total[a]) for a in span]
         for a in span:
-            residual_ref[x, a] = term[a]
+            term_ref[x, a] = term[a]
         carry = forward(x, term, carry)
         for a in span:
             swept_ref[x, a] = carry[a]
@@ -265,7 +305,8 @@
     zeroed = tuple(jnp.zeros(shape, jnp.float32) for _ in span)
     carry = lax.fori_loop(0, nx, plane, zeroed)
     for a in span:
-        scatter(sizes, out_ref, sizes.vec_rows, a, carry[a])
+        scatter(sizes, out_ref, sizes.map_rows, 3 * sizes.square + a, carry[a])
+    leave(nx - 1).start()
 
     def back(count, carry):
         x = nx - 1 - count
@@ -273,10 +314,12 @@
 
     carry = lax.fori_loop(0, nx, back, zeroed)
     for a in span:
-        scatter(sizes, out_ref, sizes.vec_rows, comps + a, carry[a])
-
-
-def chain_kernel(sizes, maps_ref, vec_ref, out_ref):
+        scatter(sizes, out_ref, sizes.map_rows, 3 * sizes.square + comps + a, carry[a])
+    for x in range(nx):
+        leave(x).wait()
+
+
+def chain_kernel(sizes, maps_ref, out_ref):
     comps, rows, square = sizes.comps, sizes.rows, sizes.square
     span = range(comps)
 
@@ -299,7 +342,7 @@
         for a in span:
             out_ref[pl.ds(part * sizes.vec_rows + a * rows, rows), :] = carry[a]
         moved = matrix(part, 0, carry)
-        carry = [moved[a] + item(vec_ref, sizes.vec_rows, part, a) for a in span]
+        carry = [moved[a] + item(maps_ref, sizes.map_rows, part, 3 * square + a) for a in span]
     carry = [jnp.zeros((rows, LANES), jnp.float32)] * comps
     for part in reversed(range(sizes.parts)):
         for a in span:
@@ -307,19 +350,25 @@
         moved = matrix(part, square, carry)
         mixed = matrix(part, 2 * square, incoming[part])
         carry = [
-            moved[a] + (mixed[a] * GROW + item(vec_ref, sizes.vec_rows, part, comps + a))
+            moved[a] + (mixed[a] * GROW + item(maps_ref, sizes.map_rows, part, 3 * square + comps + a))
             for a in span
         ]
 
 
-def finish_kernel(sizes, residual_ref, diag_ref, lower_ref, upper_ref, vec_ref, update_ref, swept_ref):
+def finish_kernel(
+    sizes, term_ref, diag_ref, lower_ref, upper_ref, vec_ref,
+    update_hbm, swept_ref, update_ref, sems,
+):
     comps, nx = sizes.comps, sizes.nx
     span = range(comps)
     forward, backward = sweep_steps(sizes, diag_ref, lower_ref, upper_ref)
     carry = tuple(gather(sizes, vec_ref, sizes.vec_rows, a) for a in span)
 
+    def leave(x):
+        return pltpu.make_async_copy(update_ref.at[x], update_hbm.at[x], sems.at[x])
+
     def ahead(x, carry):
-        carry = forward(x, [residual_ref[x, a] for a in span], carry)
+        carry = forward(x, [term_ref[x, a] for a in span], carry)
         for a in span:
             swept_ref[x, a] = carry[a]
         return tuple(carry)
@@ -329,26 +378,40 @@
 
     def back(count, carry):
         x = nx - 1 - count
+
+        @pl.when(count > 0)
+        def send():
+            leave(x + 1).start()
+
         carry = backward(x, [swept_ref[x, a] for a in span], carry)
         for a in span:
             update_ref[x, a] = carry[a]
         return tuple(carry)
 
     lax.fori_loop(0, nx, back, carry)
+    leave(0).start()
+    for x in range(nx):
+        leave(x).wait()
 
 
 VMEM = pl.BlockSpec(memory_space=pltpu.VMEM)
 SMEM = pl.BlockSpec(memory_space=pltpu.SMEM)
-
-
-def call(kernel, name, in_specs, outs, scratch, limit, flops):
+HBM = pl.BlockSpec(memory_space=pltpu.HBM)
+
+
+def floats(shape):
+    return jax.ShapeDtypeStruct(shape, jnp.float32)
+
+
+def call(kernel, name, in_specs, outs, scratch, limit, flops, out_specs=None, aliases=None):
     return pl.pallas_call(
         kernel,
         name=name,
         in_specs=in_specs,
-        out_specs=tuple(VMEM for _ in outs),
-        out_shape=tuple(jax.ShapeDtypeStruct(shape, jnp.float32) for shape in outs),
-        scratch_shapes=[pltpu.VMEM(shape, jnp.float32) for shape in scratch],
+        out_specs=tuple(out_specs or [VMEM] * len(outs)),
+        out_shape=tuple(outs),
+        scratch_shapes=scratch,
+        input_output_aliases=aliases or {},
         compiler_params=pltpu.CompilerParams(vmem_limit_bytes=limit * MIB),
         cost_estimate=pl.CostEstimate(flops=flops, bytes_accessed=1 << 20, transcendentals=0),
     )
@@ -382,51 +445,65 @@
     square = (nx, comps, comps, ny, nz)
     face = (comps, ny, nz)
     cells = nx * ny * nz
-
-    (maps,) = call(
-        functools.partial(maps_kernel, sizes), "maps", [VMEM, SMEM, SMEM],
-        [(parts * sizes.map_rows, LANES)],
-        [square, (2,) + square[1:], (2,) + square[1:]],
-        12, 1150 * cells,
-    )(diag_inverse, lower_coupling, upper_neighbour_block)
-
+    vmem = lambda shape: pltpu.VMEM(shape, jnp.float32)
+
+    moved = [
+        state_field, source, fluid_mask, cell_kind, boundary_side_number,
+        center_matrix, flux_jacobian_blocks.transpose(1, 0, 2), wall_matrix,
+        lower_coupling, upper_neighbour_block,
+    ]
+    maps, diag, *moved = call(
+        functools.partial(maps_kernel, sizes), "maps", [HBM] * (1 + len(moved)),
+        [floats((parts * sizes.map_rows, LANES)), floats(square)]
+        + [jax.ShapeDtypeStruct(array.shape, array.dtype) for array in moved],
+        [
+            vmem(square), vmem((2,) + square[1:]), vmem((2,) + square[1:]),
+            pltpu.SMEM((comps, comps), jnp.float32), pltpu.SMEM((comps, comps), jnp.float32),
+            pltpu.SemaphoreType.DMA((nx,)), pltpu.SemaphoreType.DMA((len(moved),)),
+            pltpu.SemaphoreType.DMA((2,)),
+        ],
+        16, 1150 * cells,
+    )(*(pltpu.with_memory_space_constraint(array, pltpu.HBM) for array in [diag_inverse] + moved))
+    state, source, mask, kind, side, center, flux, wall, lower, upper = moved
     y_count, z_count = (1 if gy_two else 2), (1 if gz_two else 2)
     masked, west, east, *rest = call(
         functools.partial(edges_kernel, sizes, gy_two, gz_two), "edges", [VMEM, VMEM],
-        [state_field.shape, face, face]
-        + [(nx * comps, nz)] * y_count + [(sizes.edge_rows, LANES)] * z_count,
+        [floats(state.shape), floats(face), floats(face)]
+        + [floats((nx * comps, nz))] * y_count + [floats((sizes.edge_rows, LANES))] * z_count,
         [], 8, 10 * cells,
-    )(state_field, fluid_mask)
+    )(state, mask)
     y_low, y_high = rest[0], rest[y_count - 1]
     z_low, z_high = rest[y_count], rest[y_count + z_count - 1]
 
     from_west, from_east = shifted(west, east, "gx", parts)
     from_south, from_north = shifted(y_low, y_high, "gy", gy)
     from_below, from_above = shifted(z_low, z_high, "gz", gz)
+
+    residual, term, maps = call(
+        functools.partial(residual_kernel, sizes, gy_two, gz_two), "residual",
+        [VMEM] * 6 + [SMEM] * 3 + [VMEM] + [SMEM] * 2 + [VMEM] * 7,
+        [floats(state.shape), floats(state.shape), floats(maps.shape)],
+        [
+            vmem(state.shape), vmem((sizes.edge_rows, LANES)), vmem((sizes.edge_rows, LANES)),
+            pltpu.SemaphoreType.DMA((nx,)),
+        ],
+        16, 650 * cells, [HBM, VMEM, VMEM], {18: 2},
+    )(
+        state, masked, source, mask, kind, side, center, flux, wall, diag, lower, upper,
+        from_west, from_east, from_south, from_north, from_below, from_above, maps,
+    )
     maps = spread(sizes, maps, sizes.map_rows)
-
-    residual, vectors = call(
-        functools.partial(residual_kernel, sizes, gy_two, gz_two), "residual",
-        [VMEM] * 6 + [SMEM] * 3 + [VMEM] + [SMEM] * 2 + [VMEM] * 6,
-        [state_field.shape, (parts * sizes.vec_rows, LANES)],
-        [state_field.shape, (sizes.edge_rows, LANES), (sizes.edge_rows, LANES)],
-        16, 650 * cells,
-    )(
-        state_field, masked, source, fluid_mask, cell_kind, boundary_side_number,
-        center_matrix, flux_jacobian_blocks, wall_matrix,
-        diag_inverse, lower_coupling, upper_neighbour_block,
-        from_west, from_east, from_south, from_north, from_below, from_above,
-    )
-    vectors = spread(sizes, vectors, sizes.vec_rows)
     (incoming,) = call(
-        functools.partial(chain_kernel, sizes), "chain", [VMEM, VMEM],
-        [(parts * sizes.vec_rows, LANES)], [], 4, 1200 * ny * nz,
-    )(maps, vectors)
+        functools.partial(chain_kernel, sizes), "chain", [VMEM],
+        [floats((parts * sizes.vec_rows, LANES))], [], 4, 1200 * ny * nz,
+    )(maps)
     incoming = spread(sizes, incoming, sizes.vec_rows)
     (update,) = call(
         functools.partial(finish_kernel, sizes), "finish", [VMEM, VMEM, SMEM, SMEM, VMEM],
-        [state_field.shape], [state_field.shape], 8, 200 * cells,
-    )(residual, diag_inverse, lower_coupling, upper_neighbour_block, incoming)
+        [floats(state.shape)],
+        [vmem(state.shape), vmem(state.shape), pltpu.SemaphoreType.DMA((nx,))],
+        8, 200 * cells, [HBM],
+    )(term, diag, lower, upper, incoming)
     return update, residual
 
 

time: 80.9 us -> 63.4 us (0.78)
  local copies, waits for them, and re-layouts: 14.2 us -> 0 us
  starting transfers between devices: 14.2 us -> 7.75 us
  blocking collectives: 31.6 us -> 34.5 us
    unnamed x35 -> x0, local copies, waits for them, and re-layouts: 14.2 us -> none
    all_to_all x1 -> x0, starting transfers between devices: 6.42 us -> none  [spread(): lax.all_to_all(blocks, 'gx', split_axis=0, concat_axis=0, tiled=True)]
    all_to_all x2, blocking collectives: 31.6 us -> 34.5 us  [spread(): lax.all_to_all(blocks, 'gx', split_axis=0, concat_axis=0, tiled=True)]
  transfers between devices with their start and end apart: 5 -> 4, of which waited for: 2 -> 2; matrix products, arithmetic and copies ran while one was open for 1% -> 0% of each run, Pallas kernels for 9% -> 0%
where the time goes in v2:
time: 63.4 us; the launch traced here: 63.1 us
  blocking collectives  34.5 us (54%)
  Pallas kernels  17.2 us (27%)
  starting transfers between devices  7.75 us (12%)
  waiting for transfers between devices  3.01 us (5%)
  between operations  0.68 us (1%)
    all_to_all x2, blocking collectives, spread(): lax.all_to_all(blocks, 'gx', split_axis=0, concat_axis=0, tiled=True)  34.5 us
    pallas_call x1, Pallas kernels, on_device(): call(functools.partial(maps_kernel, sizes), 'maps', [HBM] * (1 + len(move...  7.54 us
    pallas_call x1, Pallas kernels, on_device(): call(functools.partial(residual_kernel, sizes, gy_two, gz_two), 'residual...  6.58 us
    ppermute x2, starting transfers between devices, shifted(): return (lax.ppermute(high, axis, up), lax.ppermute(low, axis, down))  6.17 us
    pallas_call x1, Pallas kernels, on_device(): call(functools.partial(finish_kernel, sizes), 'finish', [VMEM, VMEM, SMEM...  2.62 us
    ppermute x2, waiting for transfers between devices, shifted(): return (lax.ppermute(high, axis, up), lax.ppermute(low, axis, down))  1.84 us
    ppermute x2, starting transfers between devices, shifted(): other = lax.ppermute(low, axis, [(0, 1), (1, 0)])  1.59 us
  transfers between devices with their start and end apart: 4, of which 2 were waited for; matrix products, arithmetic and copies ran while one was open for 0% of the time, Pallas kernels for 0%

profile of v2, /device:TPU:0, one launch (start us, length us, event | category | flops | bytes accessed | tf_op | source)
XLA Modules:
  0.0 63.1 jit_solution(6106171126753715053)
XLA Ops:
  0.6 7.5 %maps.1 = (f32[1408,128]{1,0:T(8,128)S(1)}, f32[16,5,5,16,128]{4,3,2,1,0:T(8,128)S(1)}, f32[16,5,16,128]{3,2,1,0:T(8,128)S(1)}, f32[16,5,16,128]{3,2,1,0:T(8,128...) custom-call(f32[16,5,5,16,128]{4,3,2,1,0:T(8,128)} %diag_hbm.1, ...), custom_call_target="tpu_custom_call" | custom-call | flops 37683200 | bytes 1048576 | tf_op jit(solution)/shard_map/maps/pallas_call | solution.py:455
  8.2 0.3 edges.1
  8.5 4.9 %collective-permute-start = (f32[5,16,128]{2,1,0:T(8,128)S(1)}, f32[5,16,128]{2,1,0:T(8,128)S(1)}, u32[]{:S(2)}, u32[]{:S(2)}) collective-permute-start(f32[5,16,128]{2,1,0:T(8,128)S(1)} %get-tuple-element.34), channel_id=1, source_target_pairs={{0,4},{4,8},{8,12},{12,16},{16,20},{20,24},{24,28},{1,5},{5,9},{9,... | collective-permute-start | bytes 122888 | tf_op jit(solution)/shard_map/ppermute | solution.py:426
  13.4 1.3 %collective-permute-start.1 = (f32[5,16,128]{2,1,0:T(8,128)S(1)}, f32[5,16,128]{2,1,0:T(8,128)S(1)}, u32[]{:S(2)}, u32[]{:S(2)}) collective-permute-start(f32[5,16,128]{2,1,0:T(8,128)S(1)} %get-tuple-element.35), channel_id=1, source_target_pairs={{4,0},{8,4},{12,8},{16,12},{20,16},{24,20},{28,24},{5,1},{9,5},{13... | collective-permute-start | bytes 122888 | tf_op jit(solution)/shard_map/ppermute | solution.py:426
  14.7 1.6 %collective-permute-start.2 = (f32[80,128]{1,0:T(8,128)S(1)}, f32[80,128]{1,0:T(8,128)S(1)}, u32[]{:S(2)}, u32[]{:S(2)}) collective-permute-start(f32[80,128]{1,0:T(8,128)S(1)} %get-tuple-element.36), channel_id=1, source_target_pairs={{0,2},{2,0},{1,3},{3,1},{4,6},{6,4},{5,7},{7,5},{8,10},{10,8},{9,1... | collective-permute-start | bytes 122888 | tf_op jit(solution)/shard_map/ppermute | solution.py:422
  16.2 0.0 collective-permute-start.3
  16.2 1.2 %collective-permute-done.3.below_ref.above_ref = f32[16,128]{1,0:T(8,128)S(1)} collective-permute-done((f32[16,128]{1,0:T(8,128)S(1)}, f32[16,128]{1,0:T(8,128)S(1)}, u32[]{:S(2)}, u32[]{:S(2)}) %collective-permute-start.3) | collective-permute-done | bytes 8224 | tf_op jit(solution)/shard_map/ppermute | solution.py:422
  17.4 0.0 collective-permute-done.west_ref
  17.4 1.8 %collective-permute-done.1.east_ref = f32[5,16,128]{2,1,0:T(8,128)S(1)} collective-permute-done((f32[5,16,128]{2,1,0:T(8,128)S(1)}, f32[5,16,128]{2,1,0:T(8,128)S(1)}, u32[]{:S(2)}, u32[]{:S(2)}) %collective-permute-start.1) | collective-permute-done | bytes 40992 | tf_op jit(solution)/shard_map/ppermute | solution.py:426
  19.2 0.0 collective-permute-done.2.south_ref.north_ref
  19.3 6.6 %residual.1 = (f32[16,5,16,128]{3,2,1,0:T(8,128)}, f32[16,5,16,128]{3,2,1,0:T(8,128)S(1)}, f32[1408,128]{1,0:T(8,128)S(1)}) custom-call(f32[16,5,16,128]{3,2,1,0:T(8,128)S(1)} %get-tuple-element.22.state_ref, f32[16,5,16,128]{3,2,1,0:T(8,128)S(1)} %get-tuple-element.24.masked_ref, ...), custom_call_target="tpu_custom_call", output_to_operand_aliasing={{2}: (18, {})} | custom-call | flops 21299200 | bytes 1048576 | tf_op jit(solution)/shard_map/residual/pallas_call | solution.py:482
  25.8 24.1 %all_to_all.10 = f32[8,176,128]{2,1,0:T(8,128)S(1)} all-to-all(f32[8,176,128]{2,1,0:T(8,128)S(1)} %bitcast.6), channel_id=1, replica_groups=mesh['gx'=8,'gy'=2,'gz'=2] {'gx'}, dimensions={0} | all-to-all | bytes 1441792 | tf_op jit(solution)/shard_map/all_to_all | solution.py:431
  49.9 0.2 chain.1
  50.1 10.4 %all_to_all.11 = f32[8,24,128]{2,1,0:T(8,128)S(1)} all-to-all(f32[8,24,128]{2,1,0:T(8,128)S(1)} %bitcast.7), channel_id=1, replica_groups=mesh['gx'=8,'gy'=2,'gz'=2] {'gx'}, dimensions={0} | all-to-all | bytes 196608 | tf_op jit(solution)/shard_map/all_to_all | solution.py:431
  60.5 2.6 %finish.1 = f32[16,5,16,128]{3,2,1,0:T(8,128)} custom-call(f32[16,5,16,128]{3,2,1,0:T(8,128)S(1)} %get-tuple-element.39.term_ref, f32[16,5,5,16,128]{4,3,2,1,0:T(8,128)S(1)} %get-tuple-element.31.diag_ref, f32[5,5]{1,0:T(8,128)S(1)} %get-tuple-element.32.lower_ref, f32[5,5]{1,0:T(8,128)S(1)} %get-tuple-element.33.upper_ref, f32[192,128]{1,0:T(8,128)S(1)} %bitcast.8), custom_call_target="tpu_custom_call" | custom-call | flops 6553600 | bytes 1048576 | tf_op jit(solution)/shard_map/finish/pallas_call | solution.py:501
Async XLA Ops:
  8.5 8.9 %collective-permute-start = (f32[5,16,128]{2,1,0:T(8,128)S(1)}, f32[5,16,128]{2,1,0:T(8,128)S(1)}, u32[]{:S(2)}, u32[]{:S(2)}) collective-permute-start(f32[5,16,128]{2,1,0:T(8,128)S(1)} %get-tuple-element.34), channel_id=1, source_target_pairs={{0,4},{4,8},{8,12},{12,16},{16,20},{20,24},{24,28},{1,5},{5,9},{9,... | collective-permute-start | bytes 122888 | tf_op jit(solution)/shard_map/ppermute | solution.py:426
  13.4 5.9 %collective-permute-start.1 = (f32[5,16,128]{2,1,0:T(8,128)S(1)}, f32[5,16,128]{2,1,0:T(8,128)S(1)}, u32[]{:S(2)}, u32[]{:S(2)}) collective-permute-start(f32[5,16,128]{2,1,0:T(8,128)S(1)} %get-tuple-element.35), channel_id=1, source_target_pairs={{4,0},{8,4},{12,8},{16,12},{20,16},{24,20},{28,24},{5,1},{9,5},{13... | collective-permute-start | bytes 122888 | tf_op jit(solution)/shard_map/ppermute | solution.py:426
  14.7 4.6 %collective-permute-start.2 = (f32[80,128]{1,0:T(8,128)S(1)}, f32[80,128]{1,0:T(8,128)S(1)}, u32[]{:S(2)}, u32[]{:S(2)}) collective-permute-start(f32[80,128]{1,0:T(8,128)S(1)} %get-tuple-element.36), channel_id=1, source_target_pairs={{0,2},{2,0},{1,3},{3,1},{4,6},{6,4},{5,7},{7,5},{8,10},{10,8},{9,1... | collective-permute-start | bytes 122888 | tf_op jit(solution)/shard_map/ppermute | solution.py:422
  16.2 1.2 %collective-permute-start.3 = (f32[16,128]{1,0:T(8,128)S(1)}, f32[16,128]{1,0:T(8,128)S(1)}, u32[]{:S(2)}, u32[]{:S(2)}) collective-permute-start(f32[16,128]{1,0:T(8,128)S(1)} %get-tuple-element.37), channel_id=1, source_target_pairs={{0,1},{1,0},{2,3},{3,2},{4,5},{5,4},{6,7},{7,6},{8,9},{9,8},{10,11... | collective-permute-start | bytes 24584 | tf_op jit(solution)/shard_map/ppermute | solution.py:422

commit v3 on v2

--- a/solution.py
+++ b/solution.py
@@ -51,7 +51,9 @@
     return jnp.concatenate(parts, axis=0)
 
 
-MOVED = ("state", "source", "mask", "kind", "side", "center", "flux", "wall", "lower", "upper")
+MOVED = ("state", "source", "mask", "kind", "side")
+COUPLING = ("lower", "upper")
+MATRICES = ("center", "wall", "flux")
 
 
 def combine(terms):
@@ -64,18 +66,25 @@
     return terms[0]
 
 
-def maps_kernel(
-    sizes, diag_hbm, *refs,
-):
-    count = len(MOVED)
-    sources, out_ref, diag_ref = refs[:count], refs[count], refs[count + 1]
-    targets = refs[count + 2 : 2 * count + 2]
-    fwd_ref, back_ref, mix_ref, lower_ref, upper_ref, plane_sems, sems, scalar_sems = refs[2 * count + 2 :]
+def maps_kernel(sizes, diag_hbm, *refs):
+    refs = list(refs)
+    take = lambda count: [refs.pop(0) for _ in range(count)]
+    sources = take(len(MOVED))
+    lower_hbm, upper_hbm, center_hbm, wall_hbm, flux_hbm = take(5)
+    out_ref, diag_ref, back_ref, mix_ref, table_ref = take(5)
+    targets = take(len(MOVED) + 2)
+    fwd_ref, lower_ref, upper_ref, center_ref, wall_ref, flux_ref = take(6)
+    plane_sems, sems, scalar_sems = refs
     comps, nx = sizes.comps, sizes.nx
     span = range(comps)
     scalars = [
-        pltpu.make_async_copy(sources[MOVED.index(name)], ref, scalar_sems.at[i])
-        for i, (name, ref) in enumerate((("lower", lower_ref), ("upper", upper_ref)))
+        pltpu.make_async_copy(source, target, scalar_sems.at[i])
+        for i, (source, target) in enumerate(
+            (
+                (lower_hbm, lower_ref), (upper_hbm, upper_ref), (center_hbm, center_ref),
+                (wall_hbm, wall_ref), (flux_hbm, flux_ref),
+            )
+        )
     ]
     for copy in scalars:
         copy.start()
@@ -87,59 +96,68 @@
         plane_copy(x).start()
     moves = [
         pltpu.make_async_copy(source, target, sems.at[i])
-        for i, (source, target) in enumerate(zip(sources, targets))
+        for i, (source, target) in enumerate(zip(sources + [lower_hbm, upper_hbm], targets))
     ]
     for copy in moves:
         copy.start()
     for copy in scalars:
         copy.wait()
 
-    def product(x, coupling_ref, negate):
+    for c in span:
+        for a in span:
+            entries = [center_ref[a, c], wall_ref[a, c]] + [flux_ref[a, d, c] for d in range(6)]
+            for d, entry in enumerate(entries):
+                table_ref[d, c, a] = jnp.full((SUB, LANES), entry, jnp.float32)
+
+    every = slice(None)
+    halves = [pl.ds(v * SUB, SUB) for v in range(sizes.vregs)]
+
+    def product(x, half, coupling_ref, negate):
         sign = -1.0 if negate else 1.0
         scale = [[sign * coupling_ref[b, c] for c in span] for b in span]
         rows = []
         for a in span:
-            diag = [diag_ref[x, a, b] for b in span]
+            diag = [diag_ref[x, a, b, half] for b in span]
             rows.append([combine(diag[b] * scale[b][c] for b in span) for c in span])
         return rows
 
+    def advance(step, source_ref, source_x, target_ref, target_x, half, added_ref=None):
+        for d in span:
+            column = [source_ref[source_x, c, d, half] for c in span]
+            for a in span:
+                value = combine(step[a][c] * column[c] for c in span)
+                if added_ref is not None:
+                    value = value + added_ref[target_x, a, d, half]
+                target_ref[target_x, a, d, half] = value
+
     plane_copy(0).wait()
-    first = product(0, lower_ref, False)
-    for a in span:
-        for c in span:
-            fwd_ref[0, a, c] = first[a][c] * SHRINK
+    for half in halves:
+        first = product(0, half, lower_ref, False)
+        for a in span:
+            for c in span:
+                fwd_ref[0, a, c, half] = first[a][c] * SHRINK
 
     def forward(x, carry):
         plane_copy(x).wait()
-        step = product(x, lower_ref, False)
-        for d in span:
-            column = [fwd_ref[x - 1, c, d] for c in span]
-            for a in span:
-                fwd_ref[x, a, d] = combine(step[a][c] * column[c] for c in span)
+        step = product(x, every, lower_ref, False)
+        advance(step, fwd_ref, x - 1, fwd_ref, x, every)
         return carry
 
     lax.fori_loop(1, nx, forward, 0)
 
-    last = product(nx - 1, upper_ref, True)
-    for a in span:
-        for d in span:
-            back_ref[(nx - 1) % 2, a, d] = last[a][d]
-            mix_ref[(nx - 1) % 2, a, d] = fwd_ref[nx - 1, a, d]
+    for half in halves:
+        last = product(nx - 1, half, upper_ref, True)
+        for a in span:
+            for d in span:
+                back_ref[nx - 1, a, d, half] = last[a][d]
+                mix_ref[nx - 1, a, d, half] = fwd_ref[nx - 1, a, d, half]
 
     def backward(count, carry):
         x = nx - 1 - count
-        now, before = lax.rem(x, 2), lax.rem(x + 1, 2)
-        step = product(x, upper_ref, True)
-        for d in span:
-            column = [back_ref[before, c, d] for c in span]
-            for a in span:
-                back_ref[now, a, d] = combine(step[a][c] * column[c] for c in span)
-        for d in span:
-            column = [mix_ref[before, c, d] for c in span]
-            for a in span:
-                mix_ref[now, a, d] = fwd_ref[x, a, d] + combine(
-                    step[a][c] * column[c] for c in span
-                )
+        for half in halves:
+            step = product(x, half, upper_ref, True)
+            advance(step, back_ref, x + 1, back_ref, x, half)
+            advance(step, mix_ref, x + 1, mix_ref, x, half, fwd_ref)
         return carry
 
     lax.fori_loop(1, nx, backward, 0)
@@ -215,9 +233,9 @@
 def residual_kernel(
     sizes, gy_two, gz_two,
     state_ref, masked_ref, source_ref, mask_ref, kind_ref, side_ref,
-    center_ref, flux_ref, wall_ref, diag_ref, lower_ref, upper_ref,
+    table_ref, diag_ref, lower_ref, upper_ref,
     west_ref, east_ref, south_ref, north_ref, below_ref, above_ref, maps_ref,
-    residual_hbm, term_ref, out_ref, swept_ref, zlow_ref, zhigh_ref, sems,
+    residual_hbm, update_ref, out_ref, term_ref, swept_ref, zlow_ref, zhigh_ref, sems,
 ):
     nx, comps, ny = sizes.nx, sizes.comps, sizes.ny
     span = range(comps)
@@ -239,8 +257,8 @@
         parts = []
         for v in range(sizes.vregs):
             index = (x * comps + c) * sizes.vregs + v
-            group = pl.multiple_of((index // LANES) * SUB, SUB)
-            shift = lax.rem(target + LANES - lax.rem(index, LANES), LANES)
+            group = pl.multiple_of((index >> 7) * SUB, SUB)
+            shift = (target - index) & (LANES - 1)
             parts.append(pltpu.roll(ref[pl.ds(group, SUB), :], shift, 1))
         return jnp.concatenate(parts, axis=0)
 
@@ -260,15 +278,18 @@
         open_face = [side != d for d in range(6)]
         total = [None] * comps
 
-        def add(get, c, value):
+        def add(which, c, value):
             for a in span:
-                term = get(a, c) * value
+                entry = table_ref[which, c, a]
+                term = jnp.concatenate(
+                    [entry * value[v * SUB : (v + 1) * SUB] for v in range(sizes.vregs)], axis=0
+                )
                 total[a] = term if total[a] is None else total[a] + term
 
         for c in span:
             value = state_ref[x, c]
-            add(lambda a, b: center_ref[a, b], c, value)
-            add(lambda a, b: wall_ref[a, b], c, jnp.where(walled, value, 0.0))
+            add(0, c, value)
+            add(1, c, jnp.where(walled, value, 0.0))
             masked = masked_ref[x, c]
             row = pl.ds(x * comps + c, 1)
             south = jnp.broadcast_to(south_ref[row, :], shape)
@@ -289,11 +310,7 @@
                 ),
             ]
             for d in range(6):
-                add(
-                    functools.partial(lambda e, a, b: flux_ref[a, e, b], d),
-                    c,
-                    jnp.where(open_face[d], neighbours[d], 0.0),
-                )
+                add(2 + d, c, jnp.where(open_face[d], neighbours[d], 0.0))
         term = [weight * (source_ref[x, a] - total[a]) for a in span]
         for a in span:
             term_ref[x, a] = term[a]
@@ -310,7 +327,10 @@
 
     def back(count, carry):
         x = nx - 1 - count
-        return tuple(backward(x, [swept_ref[x, a] for a in span], carry))
+        carry = backward(x, [swept_ref[x, a] for a in span], carry)
+        for a in span:
+            update_ref[x, a] = carry[a]
+        return tuple(carry)
 
     carry = lax.fori_loop(0, nx, back, zeroed)
     for a in span:
@@ -355,41 +375,28 @@
         ]
 
 
-def finish_kernel(
-    sizes, term_ref, diag_ref, lower_ref, upper_ref, vec_ref,
-    update_hbm, swept_ref, update_ref, sems,
-):
+def finish_kernel(sizes, base_ref, back_ref, mix_ref, vec_ref, update_hbm, update_ref, sems):
     comps, nx = sizes.comps, sizes.nx
     span = range(comps)
-    forward, backward = sweep_steps(sizes, diag_ref, lower_ref, upper_ref)
-    carry = tuple(gather(sizes, vec_ref, sizes.vec_rows, a) for a in span)
+    ahead = [gather(sizes, vec_ref, sizes.vec_rows, a) for a in span]
+    behind = [gather(sizes, vec_ref, sizes.vec_rows, comps + a) for a in span]
 
     def leave(x):
         return pltpu.make_async_copy(update_ref.at[x], update_hbm.at[x], sems.at[x])
 
-    def ahead(x, carry):
-        carry = forward(x, [term_ref[x, a] for a in span], carry)
-        for a in span:
-            swept_ref[x, a] = carry[a]
-        return tuple(carry)
-
-    lax.fori_loop(0, nx, ahead, carry)
-    carry = tuple(gather(sizes, vec_ref, sizes.vec_rows, comps + a) for a in span)
-
-    def back(count, carry):
-        x = nx - 1 - count
-
-        @pl.when(count > 0)
+    def plane(x, carry):
+        @pl.when(x > 0)
         def send():
-            leave(x + 1).start()
-
-        carry = backward(x, [swept_ref[x, a] for a in span], carry)
-        for a in span:
-            update_ref[x, a] = carry[a]
-        return tuple(carry)
-
-    lax.fori_loop(0, nx, back, carry)
-    leave(0).start()
+            leave(x - 1).start()
+
+        for a in span:
+            mixed = combine(mix_ref[x, a, b] * carry[b] for b in span)
+            moved = combine(back_ref[x, a, b] * carry[comps + b] for b in span)
+            update_ref[x, a] = base_ref[x, a] + (mixed * GROW + moved)
+        return carry
+
+    lax.fori_loop(0, nx, plane, tuple(ahead + behind))
+    leave(nx - 1).start()
     for x in range(nx):
         leave(x).wait()
 
@@ -447,24 +454,27 @@
     cells = nx * ny * nz
     vmem = lambda shape: pltpu.VMEM(shape, jnp.float32)
 
-    moved = [
-        state_field, source, fluid_mask, cell_kind, boundary_side_number,
-        center_matrix, flux_jacobian_blocks.transpose(1, 0, 2), wall_matrix,
-        lower_coupling, upper_neighbour_block,
-    ]
-    maps, diag, *moved = call(
-        functools.partial(maps_kernel, sizes), "maps", [HBM] * (1 + len(moved)),
-        [floats((parts * sizes.map_rows, LANES)), floats(square)]
-        + [jax.ShapeDtypeStruct(array.shape, array.dtype) for array in moved],
-        [
-            vmem(square), vmem((2,) + square[1:]), vmem((2,) + square[1:]),
-            pltpu.SMEM((comps, comps), jnp.float32), pltpu.SMEM((comps, comps), jnp.float32),
-            pltpu.SemaphoreType.DMA((nx,)), pltpu.SemaphoreType.DMA((len(moved),)),
-            pltpu.SemaphoreType.DMA((2,)),
+    moved = [state_field, source, fluid_mask, cell_kind, boundary_side_number]
+    coupling = [lower_coupling, upper_neighbour_block]
+    matrices = [center_matrix, wall_matrix, flux_jacobian_blocks.transpose(1, 0, 2)]
+    operands = [diag_inverse] + moved + coupling + matrices
+    smem = lambda shape: pltpu.SMEM(shape, jnp.float32)
+    table = (8, comps, comps, SUB, LANES)
+    maps, diag, back, mix, table, *moved = call(
+        functools.partial(maps_kernel, sizes), "maps", [HBM] * len(operands),
+        [floats((parts * sizes.map_rows, LANES)), floats(square), floats(square), floats(square)]
+        + [floats(table)]
+        + [jax.ShapeDtypeStruct(array.shape, array.dtype) for array in moved + coupling],
+        [vmem(square)]
+        + [smem(array.shape) for array in coupling + matrices]
+        + [
+            pltpu.SemaphoreType.DMA((nx,)), pltpu.SemaphoreType.DMA((len(moved + coupling),)),
+            pltpu.SemaphoreType.DMA((5,)),
         ],
-        16, 1150 * cells,
-    )(*(pltpu.with_memory_space_constraint(array, pltpu.HBM) for array in [diag_inverse] + moved))
-    state, source, mask, kind, side, center, flux, wall, lower, upper = moved
+        24, 1150 * cells,
+    )(*(pltpu.with_memory_space_constraint(array, pltpu.HBM) for array in operands))
+    state, source, mask, kind, side, lower, upper = moved
+
     y_count, z_count = (1 if gy_two else 2), (1 if gz_two else 2)
     masked, west, east, *rest = call(
         functools.partial(edges_kernel, sizes, gy_two, gz_two), "edges", [VMEM, VMEM],
@@ -479,17 +489,18 @@
     from_south, from_north = shifted(y_low, y_high, "gy", gy)
     from_below, from_above = shifted(z_low, z_high, "gz", gz)
 
-    residual, term, maps = call(
+    residual, base, maps = call(
         functools.partial(residual_kernel, sizes, gy_two, gz_two), "residual",
-        [VMEM] * 6 + [SMEM] * 3 + [VMEM] + [SMEM] * 2 + [VMEM] * 7,
+        [VMEM] * 8 + [SMEM] * 2 + [VMEM] * 7,
         [floats(state.shape), floats(state.shape), floats(maps.shape)],
         [
-            vmem(state.shape), vmem((sizes.edge_rows, LANES)), vmem((sizes.edge_rows, LANES)),
+            vmem(state.shape), vmem(state.shape),
+            vmem((sizes.edge_rows, LANES)), vmem((sizes.edge_rows, LANES)),
             pltpu.SemaphoreType.DMA((nx,)),
         ],
-        16, 650 * cells, [HBM, VMEM, VMEM], {18: 2},
+        16, 650 * cells, [HBM, VMEM, VMEM], {16: 2},
     )(
-        state, masked, source, mask, kind, side, center, flux, wall, diag, lower, upper,
+        state, masked, source, mask, kind, side, table, diag, lower, upper,
         from_west, from_east, from_south, from_north, from_below, from_above, maps,
     )
     maps = spread(sizes, maps, sizes.map_rows)
@@ -499,11 +510,11 @@
     )(maps)
     incoming = spread(sizes, incoming, sizes.vec_rows)
     (update,) = call(
-        functools.partial(finish_kernel, sizes), "finish", [VMEM, VMEM, SMEM, SMEM, VMEM],
+        functools.partial(finish_kernel, sizes), "finish", [VMEM] * 4,
         [floats(state.shape)],
-        [vmem(state.shape), vmem(state.shape), pltpu.SemaphoreType.DMA((nx,))],
-        8, 200 * cells, [HBM],
-    )(term, diag, lower, upper, incoming)
+        [vmem(state.shape), pltpu.SemaphoreType.DMA((nx,))],
+        16, 200 * cells, [HBM],
+    )(base, back, mix, incoming)
     return update, residual
 
 

time: 63.4 us -> 60.4 us (0.953)
  Pallas kernels: 17.2 us -> 14.2 us
    pallas_call x1, Pallas kernels: 6.58 us -> 4.67 us  [on_device(): call(functools.partial(residual_kernel, sizes, gy_two, gz_two), 'residual...]
    pallas_call x2, Pallas kernels: 10.2 us -> 9.04 us  [the longest x1 7.67 us: on_device(): call(functools.partial(maps_kernel, sizes), 'maps', [HBM] * len(operands)...]
where the time goes in v3:
time: 60.4 us; the launch traced here: 60.1 us
  blocking collectives  34.5 us (57%)
  Pallas kernels  14.2 us (24%)
  starting transfers between devices  7.75 us (13%)
  waiting for transfers between devices  3.01 us (5%)
  between operations  0.68 us (1%)
    all_to_all x2, blocking collectives, spread(): lax.all_to_all(blocks, 'gx', split_axis=0, concat_axis=0, tiled=True)  34.5 us
    pallas_call x1, Pallas kernels, on_device(): call(functools.partial(maps_kernel, sizes), 'maps', [HBM] * len(operands)...  7.67 us
    ppermute x2, starting transfers between devices, shifted(): return (lax.ppermute(high, axis, up), lax.ppermute(low, axis, down))  6.17 us
    pallas_call x1, Pallas kernels, on_device(): call(functools.partial(residual_kernel, sizes, gy_two, gz_two), 'residual...  4.67 us
    ppermute x2, waiting for transfers between devices, shifted(): return (lax.ppermute(high, axis, up), lax.ppermute(low, axis, down))  1.84 us
    ppermute x2, starting transfers between devices, shifted(): other = lax.ppermute(low, axis, [(0, 1), (1, 0)])  1.59 us
    pallas_call x1, Pallas kernels, on_device(): call(functools.partial(finish_kernel, sizes), 'finish', [VMEM] * 4, [floa...  1.37 us
  transfers between devices with their start and end apart: 4, of which 2 were waited for; matrix products, arithmetic and copies ran while one was open for 0% of the time, Pallas kernels for 0%

profile of v3, /device:TPU:0, one launch (start us, length us, event | category | flops | bytes accessed | tf_op | source)
XLA Modules:
  0.0 60.1 jit_solution(13381946679677748214)
XLA Ops:
  0.6 7.7 %maps.1 = (f32[1408,128]{1,0:T(8,128)S(1)}, f32[16,5,5,16,128]{4,3,2,1,0:T(8,128)S(1)}, f32[16,5,5,16,128]{4,3,2,1,0:T(8,128)S(1)}, f32[16,5,5,16,128]{4,3,2,1,0...) custom-call(f32[16,5,5,16,128]{4,3,2,1,0:T(8,128)} %diag_hbm.1, ...), custom_call_target="tpu_custom_call" | custom-call | flops 37683200 | bytes 1048576 | tf_op jit(solution)/shard_map/maps/pallas_call | solution.py:463
  8.3 0.3 edges.1
  8.6 4.9 %collective-permute-start = (f32[5,16,128]{2,1,0:T(8,128)S(1)}, f32[5,16,128]{2,1,0:T(8,128)S(1)}, u32[]{:S(2)}, u32[]{:S(2)}) collective-permute-start(f32[5,16,128]{2,1,0:T(8,128)S(1)} %get-tuple-element.32), channel_id=1, source_target_pairs={{0,4},{4,8},{8,12},{12,16},{16,20},{20,24},{24,28},{1,5},{5,9},{9,... | collective-permute-start | bytes 122888 | tf_op jit(solution)/shard_map/ppermute | solution.py:433
  13.5 1.3 %collective-permute-start.1 = (f32[5,16,128]{2,1,0:T(8,128)S(1)}, f32[5,16,128]{2,1,0:T(8,128)S(1)}, u32[]{:S(2)}, u32[]{:S(2)}) collective-permute-start(f32[5,16,128]{2,1,0:T(8,128)S(1)} %get-tuple-element.33), channel_id=1, source_target_pairs={{4,0},{8,4},{12,8},{16,12},{20,16},{24,20},{28,24},{5,1},{9,5},{13... | collective-permute-start | bytes 122888 | tf_op jit(solution)/shard_map/ppermute | solution.py:433
  14.8 1.6 %collective-permute-start.2 = (f32[80,128]{1,0:T(8,128)S(1)}, f32[80,128]{1,0:T(8,128)S(1)}, u32[]{:S(2)}, u32[]{:S(2)}) collective-permute-start(f32[80,128]{1,0:T(8,128)S(1)} %get-tuple-element.34), channel_id=1, source_target_pairs={{0,2},{2,0},{1,3},{3,1},{4,6},{6,4},{5,7},{7,5},{8,10},{10,8},{9,1... | collective-permute-start | bytes 122888 | tf_op jit(solution)/shard_map/ppermute | solution.py:429
  16.4 0.0 collective-permute-start.3
  16.4 1.2 %collective-permute-done.3.below_ref.above_ref = f32[16,128]{1,0:T(8,128)S(1)} collective-permute-done((f32[16,128]{1,0:T(8,128)S(1)}, f32[16,128]{1,0:T(8,128)S(1)}, u32[]{:S(2)}, u32[]{:S(2)}) %collective-permute-start.3) | collective-permute-done | bytes 8224 | tf_op jit(solution)/shard_map/ppermute | solution.py:429
  17.5 0.0 collective-permute-done.west_ref
  17.6 1.8 %collective-permute-done.1.east_ref = f32[5,16,128]{2,1,0:T(8,128)S(1)} collective-permute-done((f32[5,16,128]{2,1,0:T(8,128)S(1)}, f32[5,16,128]{2,1,0:T(8,128)S(1)}, u32[]{:S(2)}, u32[]{:S(2)}) %collective-permute-start.1) | collective-permute-done | bytes 40992 | tf_op jit(solution)/shard_map/ppermute | solution.py:433
  19.4 0.0 collective-permute-done.2.south_ref.north_ref
  19.4 4.7 %residual.1 = (f32[16,5,16,128]{3,2,1,0:T(8,128)}, f32[16,5,16,128]{3,2,1,0:T(8,128)S(1)}, f32[1408,128]{1,0:T(8,128)S(1)}) custom-call(f32[16,5,16,128]{3,2,1,0:T(8,128)S(1)} %get-tuple-element.22.state_ref, f32[16,5,16,128]{3,2,1,0:T(8,128)S(1)} %get-tuple-element.24.masked_ref, ...), custom_call_target="tpu_custom_call", output_to_operand_aliasing={{2}: (16, {})} | custom-call | flops 21299200 | bytes 1048576 | tf_op jit(solution)/shard_map/residual/pallas_call | solution.py:492
  24.1 24.1 %all_to_all.10 = f32[8,176,128]{2,1,0:T(8,128)S(1)} all-to-all(f32[8,176,128]{2,1,0:T(8,128)S(1)} %bitcast.6), channel_id=1, replica_groups=mesh['gx'=8,'gy'=2,'gz'=2] {'gx'}, dimensions={0} | all-to-all | bytes 1441792 | tf_op jit(solution)/shard_map/all_to_all | solution.py:438
  48.1 0.2 chain.1
  48.3 10.4 %all_to_all.11 = f32[8,24,128]{2,1,0:T(8,128)S(1)} all-to-all(f32[8,24,128]{2,1,0:T(8,128)S(1)} %bitcast.8), channel_id=1, replica_groups=mesh['gx'=8,'gy'=2,'gz'=2] {'gx'}, dimensions={0} | all-to-all | bytes 196608 | tf_op jit(solution)/shard_map/all_to_all | solution.py:438
  58.7 1.4 %finish.1 = f32[16,5,16,128]{3,2,1,0:T(8,128)} custom-call(f32[16,5,16,128]{3,2,1,0:T(8,128)S(1)} %get-tuple-element.37.base_ref, f32[16,5,5,16,128]{4,3,2,1,0:T(8,128)S(1)} %get-tuple-element.38.back_ref, f32[16,5,5,16,128]{4,3,2,1,0:T(8,128)S(1)} %get-tuple-element.39.mix_ref, f32[192,128]{1,0:T(8,128)S(1)} %bitcast.7), custom_call_target="tpu_custom_call" | custom-call | flops 6553600 | bytes 1048576 | tf_op jit(solution)/shard_map/finish/pallas_call | solution.py:512
Async XLA Ops:
  8.6 8.9 %collective-permute-start = (f32[5,16,128]{2,1,0:T(8,128)S(1)}, f32[5,16,128]{2,1,0:T(8,128)S(1)}, u32[]{:S(2)}, u32[]{:S(2)}) collective-permute-start(f32[5,16,128]{2,1,0:T(8,128)S(1)} %get-tuple-element.32), channel_id=1, source_target_pairs={{0,4},{4,8},{8,12},{12,16},{16,20},{20,24},{24,28},{1,5},{5,9},{9,... | collective-permute-start | bytes 122888 | tf_op jit(solution)/shard_map/ppermute | solution.py:433
  13.5 5.9 %collective-permute-start.1 = (f32[5,16,128]{2,1,0:T(8,128)S(1)}, f32[5,16,128]{2,1,0:T(8,128)S(1)}, u32[]{:S(2)}, u32[]{:S(2)}) collective-permute-start(f32[5,16,128]{2,1,0:T(8,128)S(1)} %get-tuple-element.33), channel_id=1, source_target_pairs={{4,0},{8,4},{12,8},{16,12},{20,16},{24,20},{28,24},{5,1},{9,5},{13... | collective-permute-start | bytes 122888 | tf_op jit(solution)/shard_map/ppermute | solution.py:433
  14.8 4.6 %collective-permute-start.2 = (f32[80,128]{1,0:T(8,128)S(1)}, f32[80,128]{1,0:T(8,128)S(1)}, u32[]{:S(2)}, u32[]{:S(2)}) collective-permute-start(f32[80,128]{1,0:T(8,128)S(1)} %get-tuple-element.34), channel_id=1, source_target_pairs={{0,2},{2,0},{1,3},{3,1},{4,6},{6,4},{5,7},{7,5},{8,10},{10,8},{9,1... | collective-permute-start | bytes 122888 | tf_op jit(solution)/shard_map/ppermute | solution.py:429
  16.4 1.2 %collective-permute-start.3 = (f32[16,128]{1,0:T(8,128)S(1)}, f32[16,128]{1,0:T(8,128)S(1)}, u32[]{:S(2)}, u32[]{:S(2)}) collective-permute-start(f32[16,128]{1,0:T(8,128)S(1)} %get-tuple-element.35), channel_id=1, source_target_pairs={{0,1},{1,0},{2,3},{3,2},{4,5},{5,4},{6,7},{7,6},{8,9},{9,8},{10,11... | collective-permute-start | bytes 24584 | tf_op jit(solution)/shard_map/ppermute | solution.py:429

commit v4 on v3

--- a/solution.py
+++ b/solution.py
@@ -23,31 +23,38 @@
         self.nx, self.comps, self.ny, self.nz = state_shape
         self.parts = lax.axis_size("gx")
         self.vregs = self.ny // SUB
-        self.rows = self.ny // self.parts
-        assert self.nz == LANES and self.parts % SUB == 0
-        assert self.ny % self.parts == 0
+        self.rows = SUB // 2
+        self.group = self.ny // self.rows
+        assert self.nz == LANES and self.ny % SUB == 0 and self.parts % 2 == 0
+        assert self.parts % self.group == 0
         self.square = self.comps * self.comps
-        self.map_rows = round_up((3 * self.square + 2 * self.comps) * self.rows, SUB)
-        self.vec_rows = round_up(2 * self.comps * self.rows, SUB)
+        self.vectors = 2 * self.comps
+        self.chunk = round_up((self.vectors + 3 * self.square) * self.rows, SUB)
+        self.vec_rows = round_up(self.vectors * self.rows, SUB)
+        self.hop_rows = round_up(self.comps * self.rows, SUB)
         self.edge_count = self.nx * self.comps * self.vregs
         self.edge_rows = SUB * -(-self.edge_count // LANES)
 
-    def start(self, index, vreg, chunk):
-        first = vreg * SUB
-        return (first % self.parts) * chunk + index * self.rows + first // self.parts
-
-
-def scatter(sizes, ref, chunk, index, value):
-    for vreg in range(sizes.vregs):
-        start = sizes.start(index, vreg, chunk)
-        ref[pl.ds(start, SUB, stride=chunk), :] = value[vreg * SUB : (vreg + 1) * SUB]
-
-
-def gather(sizes, ref, chunk, index):
+
+def scatter(sizes, ref, index, values):
+    half = SUB // 2
+    low = lax.broadcasted_iota(jnp.int32, (SUB, LANES), 0) < half
+    for i in range(0, len(values), 2):
+        first, second = values[i], values[min(i + 1, len(values) - 1)]
+        for v in range(sizes.vregs):
+            one, two = (value[v * SUB : (v + 1) * SUB] for value in (first, second))
+            start = 2 * v * sizes.chunk + (index + i) * half
+            ref[start : start + SUB, :] = jnp.where(low, one, pltpu.roll(two, half, 0))
+            start += sizes.chunk
+            ref[start : start + SUB, :] = jnp.where(low, pltpu.roll(one, half, 0), two)
+
+
+def gather(sizes, ref, index):
+    half = SUB // 2
     parts = []
-    for vreg in range(sizes.vregs):
-        start = sizes.start(index, vreg, chunk)
-        parts.append(ref[pl.ds(start, SUB, stride=chunk), :])
+    for part in range(sizes.group):
+        start = part * sizes.vec_rows + index * half
+        parts.append(ref[start : start + half, :])
     return jnp.concatenate(parts, axis=0)
 
 
@@ -162,18 +169,19 @@
 
     lax.fori_loop(1, nx, backward, 0)
 
-    for a in span:
-        for d in span:
-            index = a * comps + d
-            scatter(sizes, out_ref, sizes.map_rows, index, fwd_ref[nx - 1, a, d] * GROW)
-            scatter(sizes, out_ref, sizes.map_rows, sizes.square + index, back_ref[0, a, d])
-            scatter(sizes, out_ref, sizes.map_rows, 2 * sizes.square + index, mix_ref[0, a, d])
+    pairs = [(a, d) for a in span for d in span]
+    scatter(
+        sizes, out_ref, sizes.vectors,
+        [fwd_ref[nx - 1, a, d] * GROW for a, d in pairs]
+        + [back_ref[0, a, d] for a, d in pairs]
+        + [mix_ref[0, a, d] for a, d in pairs],
+    )
     for copy in moves:
         copy.wait()
 
 
 def edges_kernel(sizes, gy_two, gz_two, state_ref, mask_ref, *refs):
-    masked_ref, west_ref, east_ref, *rest = refs
+    masked_ref, inner_ref, outer_ref, *rest = refs
     y_refs = rest[: 1 if gy_two else 2]
     z_refs = rest[len(y_refs) :]
     nx, comps = sizes.nx, sizes.comps
@@ -182,15 +190,18 @@
     shifts = [low_z] if gz_two else [0, 1]
     packed = [[jnp.zeros((SUB, LANES), jnp.float32)] * (sizes.edge_rows // SUB) for _ in shifts]
     low_y = lax.axis_index("gy") == 0
+    even = lax.rem(lax.axis_index("gx"), 2) == 0
+    first = []
     for x in range(nx):
         fluid = mask_ref[x].astype(jnp.float32)
         for c in range(comps):
             value = state_ref[x, c] * fluid
             masked_ref[x, c] = value
             if x == 0:
-                west_ref[c] = value
+                first.append(value)
             if x == nx - 1:
-                east_ref[c] = value
+                inner_ref[c] = jnp.where(even, value, first[c])
+                outer_ref[c] = jnp.where(even, first[c], value)
             row = pl.ds(x * comps + c, 1)
             bottom, top = value[0:1], value[sizes.ny - 1 : sizes.ny]
             if gy_two:
@@ -234,8 +245,9 @@
     sizes, gy_two, gz_two,
     state_ref, masked_ref, source_ref, mask_ref, kind_ref, side_ref,
     table_ref, diag_ref, lower_ref, upper_ref,
-    west_ref, east_ref, south_ref, north_ref, below_ref, above_ref, maps_ref,
-    residual_hbm, update_ref, out_ref, term_ref, swept_ref, zlow_ref, zhigh_ref, sems,
+    inner_ref, outer_ref, south_ref, north_ref, below_ref, above_ref, maps_ref,
+    residual_hbm, update_ref, out_ref,
+    term_ref, swept_ref, zlow_ref, zhigh_ref, west_ref, east_ref, sems,
 ):
     nx, comps, ny = sizes.nx, sizes.comps, sizes.ny
     span = range(comps)
@@ -251,6 +263,11 @@
         above = jnp.where(low_z, above, 0.0)
     zlow_ref[...] = below
     zhigh_ref[...] = above
+    even = lax.rem(lax.axis_index("gx"), 2) == 0
+    for c in span:
+        inner, outer = inner_ref[c], outer_ref[c]
+        west_ref[c] = jnp.where(even, outer, inner)
+        east_ref[c] = jnp.where(even, inner, outer)
     forward, backward = sweep_steps(sizes, diag_ref, lower_ref, upper_ref)
 
     def edge_column(ref, x, c, target):
@@ -320,9 +337,7 @@
         return tuple(carry)
 
     zeroed = tuple(jnp.zeros(shape, jnp.float32) for _ in span)
-    carry = lax.fori_loop(0, nx, plane, zeroed)
-    for a in span:
-        scatter(sizes, out_ref, sizes.map_rows, 3 * sizes.square + a, carry[a])
+    ahead = lax.fori_loop(0, nx, plane, zeroed)
     leave(nx - 1).start()
 
     def back(count, carry):
@@ -332,54 +347,82 @@
             update_ref[x, a] = carry[a]
         return tuple(carry)
 
-    carry = lax.fori_loop(0, nx, back, zeroed)
-    for a in span:
-        scatter(sizes, out_ref, sizes.map_rows, 3 * sizes.square + comps + a, carry[a])
+    behind = lax.fori_loop(0, nx, back, zeroed)
+    scatter(sizes, out_ref, 0, list(ahead) + list(behind))
     for x in range(nx):
         leave(x).wait()
 
 
-def chain_kernel(sizes, maps_ref, out_ref):
+def chain(sizes, maps_ref):
     comps, rows, square = sizes.comps, sizes.rows, sizes.square
     span = range(comps)
 
-    def item(ref, chunk, part, index):
-        return ref[pl.ds(part * chunk + index * rows, rows), :]
-
-    def matrix(part, base, vector):
-        return [
-            combine(
-                item(maps_ref, sizes.map_rows, part, base + a * comps + b) * vector[b]
-                for b in span
-            )
-            for a in span
-        ]
-
-    carry = [jnp.zeros((rows, LANES), jnp.float32)] * comps
-    incoming = []
-    for part in range(sizes.parts):
-        incoming.append(carry)
-        for a in span:
-            out_ref[pl.ds(part * sizes.vec_rows + a * rows, rows), :] = carry[a]
-        moved = matrix(part, 0, carry)
-        carry = [moved[a] + item(maps_ref, sizes.map_rows, part, 3 * square + a) for a in span]
-    carry = [jnp.zeros((rows, LANES), jnp.float32)] * comps
-    for part in reversed(range(sizes.parts)):
-        for a in span:
-            out_ref[pl.ds(part * sizes.vec_rows + (comps + a) * rows, rows), :] = carry[a]
-        moved = matrix(part, square, carry)
-        mixed = matrix(part, 2 * square, incoming[part])
-        carry = [
-            moved[a] + (mixed[a] * GROW + item(maps_ref, sizes.map_rows, part, 3 * square + comps + a))
-            for a in span
-        ]
+    def item(part, index):
+        start = part * sizes.chunk + index * rows
+        return maps_ref[start : start + rows, :]
+
+    def matrix(part, which, vector):
+        base = sizes.vectors + which * square
+        return [combine(item(part, base + a * comps + b) * vector[b] for b in span) for a in span]
+
+    def ahead(carry):
+        entering = []
+        for part in range(sizes.group):
+            entering.append(carry)
+            moved = matrix(part, 0, carry)
+            carry = [moved[a] + item(part, a) for a in span]
+        return entering, carry
+
+    def behind(carry, ahead_entering):
+        entering = []
+        for part in reversed(range(sizes.group)):
+            entering.insert(0, carry)
+            moved = matrix(part, 1, carry)
+            mixed = matrix(part, 2, ahead_entering[part])
+            carry = [moved[a] + (mixed[a] * GROW + item(part, comps + a)) for a in span]
+        return entering, carry
+
+    return ahead, behind
+
+
+def hop_values(sizes, ref):
+    rows = sizes.rows
+    return [ref[a * rows : (a + 1) * rows, :] for a in range(sizes.comps)]
+
+
+def hop_store(sizes, ref, values):
+    for a, value in enumerate(values):
+        ref[a * sizes.rows : (a + 1) * sizes.rows, :] = value
+
+
+def ahead_kernel(sizes, entered, maps_ref, *refs):
+    *in_refs, out_ref = refs
+    zero = [jnp.zeros((sizes.rows, LANES), jnp.float32)] * sizes.comps
+    ahead, behind = chain(sizes, maps_ref)
+    hop_store(sizes, out_ref, ahead(hop_values(sizes, in_refs[0]) if entered else zero)[1])
+
+
+def behind_kernel(sizes, entered, last, maps_ref, ahead_ref, *refs):
+    *in_refs, out_ref = refs
+    zero = [jnp.zeros((sizes.rows, LANES), jnp.float32)] * sizes.comps
+    ahead, behind = chain(sizes, maps_ref)
+    forward, unused = ahead(hop_values(sizes, ahead_ref) if ahead_ref is not None else zero)
+    backward, leaving = behind(hop_values(sizes, in_refs[0]) if entered else zero, forward)
+    if not last:
+        hop_store(sizes, out_ref, leaving)
+        return
+    rows = sizes.rows
+    for part in range(sizes.group):
+        for i, value in enumerate(forward[part] + backward[part]):
+            start = part * sizes.vec_rows + i * rows
+            out_ref[start : start + rows, :] = value
 
 
 def finish_kernel(sizes, base_ref, back_ref, mix_ref, vec_ref, update_hbm, update_ref, sems):
     comps, nx = sizes.comps, sizes.nx
     span = range(comps)
-    ahead = [gather(sizes, vec_ref, sizes.vec_rows, a) for a in span]
-    behind = [gather(sizes, vec_ref, sizes.vec_rows, comps + a) for a in span]
+    ahead = [gather(sizes, vec_ref, a) for a in span]
+    behind = [gather(sizes, vec_ref, comps + a) for a in span]
 
     def leave(x):
         return pltpu.make_async_copy(update_ref.at[x], update_hbm.at[x], sems.at[x])
@@ -433,10 +476,51 @@
     return lax.ppermute(high, axis, up), lax.ppermute(low, axis, down)
 
 
+def swapped(inner, outer, count):
+    pairs = lambda first: [(i, i + 1) for i in range(first, count - 1, 2)]
+    both = lambda first: pairs(first) + [(target, origin) for origin, target in pairs(first)]
+    return lax.ppermute(inner, "gx", both(0)), lax.ppermute(outer, "gx", both(1))
+
+
 def spread(sizes, array, chunk):
-    blocks = array.reshape(sizes.parts, chunk, LANES)
-    moved = lax.all_to_all(blocks, "gx", split_axis=0, concat_axis=0, tiled=True)
+    blocks = array.reshape(sizes.group, chunk, LANES)
+    groups = [
+        list(range(first, first + sizes.group)) for first in range(0, sizes.parts, sizes.group)
+    ]
+    moved = lax.all_to_all(
+        blocks, "gx", split_axis=0, concat_axis=0, tiled=True, axis_index_groups=groups
+    )
     return moved.reshape(array.shape)
+
+
+def solve_chain(sizes, maps):
+    hop = floats((sizes.hop_rows, LANES))
+    up = [(i, i + sizes.group) for i in range(sizes.parts - sizes.group)]
+    down = [(target, origin) for origin, target in up]
+    flops = 300 * sizes.group * sizes.rows * LANES
+    steps = sizes.parts // sizes.group - 1
+    ahead = []
+    for step in range(steps):
+        (leaving,) = call(
+            functools.partial(ahead_kernel, sizes, bool(ahead)), "ahead",
+            [VMEM] * (1 + len(ahead)), [hop], [], 4, flops,
+        )(maps, *ahead)
+        ahead = [lax.ppermute(leaving, "gx", up)]
+    behind = []
+    for step in range(steps + 1):
+        last = step == steps
+        kernel = functools.partial(behind_kernel, sizes, bool(behind), last)
+        if not ahead:
+            kernel = functools.partial(
+                lambda inner, maps_ref, *refs: inner(maps_ref, None, *refs), kernel
+            )
+        out = floats((sizes.group * sizes.vec_rows, LANES)) if last else hop
+        (leaving,) = call(
+            kernel, "behind", [VMEM] * (1 + len(ahead) + len(behind)), [out], [], 4, flops
+        )(maps, *ahead, *behind)
+        if not last:
+            behind = [lax.ppermute(leaving, "gx", down)]
+    return leaving
 
 
 def on_device(
@@ -462,7 +546,7 @@
     table = (8, comps, comps, SUB, LANES)
     maps, diag, back, mix, table, *moved = call(
         functools.partial(maps_kernel, sizes), "maps", [HBM] * len(operands),
-        [floats((parts * sizes.map_rows, LANES)), floats(square), floats(square), floats(square)]
+        [floats((sizes.group * sizes.chunk, LANES)), floats(square), floats(square), floats(square)]
         + [floats(table)]
         + [jax.ShapeDtypeStruct(array.shape, array.dtype) for array in moved + coupling],
         [vmem(square)]
@@ -476,7 +560,7 @@
     state, source, mask, kind, side, lower, upper = moved
 
     y_count, z_count = (1 if gy_two else 2), (1 if gz_two else 2)
-    masked, west, east, *rest = call(
+    masked, inner, outer, *rest = call(
         functools.partial(edges_kernel, sizes, gy_two, gz_two), "edges", [VMEM, VMEM],
         [floats(state.shape), floats(face), floats(face)]
         + [floats((nx * comps, nz))] * y_count + [floats((sizes.edge_rows, LANES))] * z_count,
@@ -485,7 +569,7 @@
     y_low, y_high = rest[0], rest[y_count - 1]
     z_low, z_high = rest[y_count], rest[y_count + z_count - 1]
 
-    from_west, from_east = shifted(west, east, "gx", parts)
+    from_inner, from_outer = swapped(inner, outer, parts)
     from_south, from_north = shifted(y_low, y_high, "gy", gy)
     from_below, from_above = shifted(z_low, z_high, "gz", gz)
 
@@ -496,19 +580,16 @@
         [
             vmem(state.shape), vmem(state.shape),
             vmem((sizes.edge_rows, LANES)), vmem((sizes.edge_rows, LANES)),
+            vmem(face), vmem(face),
             pltpu.SemaphoreType.DMA((nx,)),
         ],
         16, 650 * cells, [HBM, VMEM, VMEM], {16: 2},
     )(
         state, masked, source, mask, kind, side, table, diag, lower, upper,
-        from_west, from_east, from_south, from_north, from_below, from_above, maps,
+        from_inner, from_outer, from_south, from_north, from_below, from_above, maps,
     )
-    maps = spread(sizes, maps, sizes.map_rows)
-    (incoming,) = call(
-        functools.partial(chain_kernel, sizes), "chain", [VMEM],
-        [floats((parts * sizes.vec_rows, LANES))], [], 4, 1200 * ny * nz,
-    )(maps)
-    incoming = spread(sizes, incoming, sizes.vec_rows)
+    maps = spread(sizes, maps, sizes.chunk)
+    incoming = spread(sizes, solve_chain(sizes, maps), sizes.vec_rows)
     (update,) = call(
         functools.partial(finish_kernel, sizes), "finish", [VMEM] * 4,
         [floats(state.shape)],

time: 60.4 us -> 57.4 us (0.950)
  blocking collectives: 34.5 us -> 23.3 us
  waiting for transfers between devices: 3.01 us -> 9.05 us
  starting transfers between devices: 7.75 us -> 10 us
    all_to_all x2, blocking collectives: 34.5 us -> 23.3 us  [spread(): lax.all_to_all(blocks, 'gx', split_axis=0, concat_axis=0, tiled=True, axi...]
    ppermute x2 -> x4, waiting for transfers between devices: 1.84 us -> 6.58 us  [the longest x1 5.19 us: solve_chain(): behind = [lax.ppermute(leaving, 'gx', down)]]
    ppermute x2 -> x4, starting transfers between devices: 6.17 us -> 8.46 us  [the longest x1 3.48 us: solve_chain(): ahead = [lax.ppermute(leaving, 'gx', up)]]
    ppermute x2, waiting for transfers between devices: 1.17 us -> 2.47 us  [shifted(): other = lax.ppermute(low, axis, [(0, 1), (1, 0)])]
  transfers between devices with their start and end apart: 4 -> 6, of which waited for: 2 -> 4; matrix products, arithmetic and copies ran while one was open for 0% -> 0% of each run, Pallas kernels for 0% -> 0%
where the time goes in v4:
time: 57.4 us; the launch traced here: 57.1 us
  blocking collectives  23.3 us (41%)
  Pallas kernels  14 us (24%)
  starting transfers between devices  10 us (17%)
  waiting for transfers between devices  9.05 us (16%)
  between operations  0.69 us (1%)
    all_to_all x2, blocking collectives, spread(): lax.all_to_all(blocks, 'gx', split_axis=0, concat_axis=0, tiled=True, axi...  23.3 us
    pallas_call x1, Pallas kernels, on_device(): call(functools.partial(maps_kernel, sizes), 'maps', [HBM] * len(operands)...  7.52 us
    ppermute x1, waiting for transfers between devices, solve_chain(): behind = [lax.ppermute(leaving, 'gx', down)]  5.19 us
    pallas_call x1, Pallas kernels, on_device(): call(functools.partial(residual_kernel, sizes, gy_two, gz_two), 'residual...  4.63 us
    ppermute x1, starting transfers between devices, solve_chain(): ahead = [lax.ppermute(leaving, 'gx', up)]  3.48 us
    ppermute x1, starting transfers between devices, swapped(): lax.ppermute(inner, 'gx', both(0))  3.03 us
    ppermute x2, waiting for transfers between devices, shifted(): other = lax.ppermute(low, axis, [(0, 1), (1, 0)])  2.47 us
    ppermute x2, starting transfers between devices, shifted(): other = lax.ppermute(low, axis, [(0, 1), (1, 0)])  1.59 us
  transfers between devices with their start and end apart: 6, of which 4 were waited for; matrix products, arithmetic and copies ran while one was open for 0% of the time, Pallas kernels for 0%

profile of v4, /device:TPU:0, one launch (start us, length us, event | category | flops | bytes accessed | tf_op | source)
XLA Modules:
  0.0 57.1 jit_solution(16587270213796858298)
XLA Ops:
  0.6 7.5 %maps.1 = (f32[1376,128]{1,0:T(8,128)S(1)}, f32[16,5,5,16,128]{4,3,2,1,0:T(8,128)S(1)}, f32[16,5,5,16,128]{4,3,2,1,0:T(8,128)S(1)}, f32[16,5,5,16,128]{4,3,2,1,0...) custom-call(f32[16,5,5,16,128]{4,3,2,1,0:T(8,128)} %diag_hbm.1, ...), custom_call_target="tpu_custom_call" | custom-call | flops 37683200 | bytes 1048576 | tf_op jit(solution)/shard_map/maps/pallas_call | solution.py:547
  8.2 0.3 edges.1
  8.5 3.0 %collective-permute-start = (f32[5,16,128]{2,1,0:T(8,128)S(1)}, f32[5,16,128]{2,1,0:T(8,128)S(1)}, u32[]{:S(2)}, u32[]{:S(2)}) collective-permute-start(f32[5,16,128]{2,1,0:T(8,128)S(1)} %get-tuple-element.32), channel_id=1, source_target_pairs={{0,4},{8,12},{16,20},{24,28},{4,0},{12,8},{20,16},{28,24},{1,5},{9... | collective-permute-start | bytes 122888 | tf_op jit(solution)/shard_map/ppermute | solution.py:482
  11.5 0.7 %collective-permute-start.1 = (f32[5,16,128]{2,1,0:T(8,128)S(1)}, f32[5,16,128]{2,1,0:T(8,128)S(1)}, u32[]{:S(2)}, u32[]{:S(2)}) collective-permute-start(f32[5,16,128]{2,1,0:T(8,128)S(1)} %get-tuple-element.33), channel_id=1, source_target_pairs={{4,8},{12,16},{20,24},{8,4},{16,12},{24,20},{5,9},{13,17},{21,25},... | collective-permute-start | bytes 122888 | tf_op jit(solution)/shard_map/ppermute | solution.py:482
  12.1 1.6 %collective-permute-start.2 = (f32[80,128]{1,0:T(8,128)S(1)}, f32[80,128]{1,0:T(8,128)S(1)}, u32[]{:S(2)}, u32[]{:S(2)}) collective-permute-start(f32[80,128]{1,0:T(8,128)S(1)} %get-tuple-element.34), channel_id=1, source_target_pairs={{0,2},{2,0},{1,3},{3,1},{4,6},{6,4},{5,7},{7,5},{8,10},{10,8},{9,1... | collective-permute-start | bytes 122888 | tf_op jit(solution)/shard_map/ppermute | solution.py:472
  13.7 0.0 collective-permute-start.3
  13.7 1.2 %collective-permute-done.3.below_ref.above_ref = f32[16,128]{1,0:T(8,128)S(1)} collective-permute-done((f32[16,128]{1,0:T(8,128)S(1)}, f32[16,128]{1,0:T(8,128)S(1)}, u32[]{:S(2)}, u32[]{:S(2)}) %collective-permute-start.3) | collective-permute-done | bytes 8224 | tf_op jit(solution)/shard_map/ppermute | solution.py:472
  14.9 0.0 collective-permute-done.inner_ref
  14.9 0.0 collective-permute-done.1.outer_ref
  14.9 1.3 %collective-permute-done.2.south_ref.north_ref = f32[80,128]{1,0:T(8,128)S(1)} collective-permute-done((f32[80,128]{1,0:T(8,128)S(1)}, f32[80,128]{1,0:T(8,128)S(1)}, u32[]{:S(2)}, u32[]{:S(2)}) %collective-permute-start.2) | collective-permute-done | bytes 40992 | tf_op jit(solution)/shard_map/ppermute | solution.py:472
  16.2 4.6 %residual.1 = (f32[16,5,16,128]{3,2,1,0:T(8,128)}, f32[16,5,16,128]{3,2,1,0:T(8,128)S(1)}, f32[1376,128]{1,0:T(8,128)S(1)}) custom-call(f32[16,5,16,128]{3,2,1,0:T(8,128)S(1)} %get-tuple-element.22.state_ref, f32[16,5,16,128]{3,2,1,0:T(8,128)S(1)} %get-tuple-element.24.masked_ref, ...), custom_call_target="tpu_custom_call", output_to_operand_aliasing={{2}: (16, {})} | custom-call | flops 21299200 | bytes 1048576 | tf_op jit(solution)/shard_map/residual/pallas_call | solution.py:576
  20.9 16.1 %all_to_all.10 = f32[4,344,128]{2,1,0:T(8,128)S(1)} all-to-all(f32[4,344,128]{2,1,0:T(8,128)S(1)} %bitcast.8), channel_id=1, replica_groups={{0,4,8,12},{16,20,24,28},{1,5,9,13},{17,21,25,29},{2,6,10,14},{18,22,26..., dimensions={0} | all-to-all | bytes 1409024 | tf_op jit(solution)/shard_map/all_to_all | solution.py:490
  37.0 3.5 %collective-permute-start.4 = (f32[24,128]{1,0:T(8,128)S(1)}, f32[24,128]{1,0:T(8,128)S(1)}, u32[]{:S(2)}, u32[]{:S(2)}) collective-permute-start(f32[24,128]{1,0:T(8,128)S(1)} %ahead.1), channel_id=1, source_target_pairs={{0,16},{4,20},{8,24},{12,28},{1,17},{5,21},{9,25},{13,29},{2,18},{... | collective-permute-start | bytes 36872 | tf_op jit(solution)/shard_map/ppermute | solution.py:508
  40.5 1.4 %collective-permute-done.4.ahead_ref = f32[24,128]{1,0:T(8,128)S(1)} collective-permute-done((f32[24,128]{1,0:T(8,128)S(1)}, f32[24,128]{1,0:T(8,128)S(1)}, u32[]{:S(2)}, u32[]{:S(2)}) %collective-permute-start.4) | collective-permute-done | bytes 12320 | tf_op jit(solution)/shard_map/ppermute | solution.py:508
  41.9 0.1 behind.2
  41.9 1.3 %collective-permute-start.5 = (f32[24,128]{1,0:T(8,128)S(1)}, f32[24,128]{1,0:T(8,128)S(1)}, u32[]{:S(2)}, u32[]{:S(2)}) collective-permute-start(f32[24,128]{1,0:T(8,128)S(1)} %behind.2), channel_id=1, source_target_pairs={{16,0},{20,4},{24,8},{28,12},{17,1},{21,5},{25,9},{29,13},{18,2},{... | collective-permute-start | bytes 36872 | tf_op jit(solution)/shard_map/ppermute | solution.py:522
  43.2 5.2 %collective-permute-done.5.refs_0_ = f32[24,128]{1,0:T(8,128)S(1)} collective-permute-done((f32[24,128]{1,0:T(8,128)S(1)}, f32[24,128]{1,0:T(8,128)S(1)}, u32[]{:S(2)}, u32[]{:S(2)}) %collective-permute-start.5) | collective-permute-done | bytes 12320 | tf_op jit(solution)/shard_map/ppermute | solution.py:522
  48.4 0.1 behind.3
  48.5 7.3 %all_to_all.11 = f32[4,40,128]{2,1,0:T(8,128)S(1)} all-to-all(f32[4,40,128]{2,1,0:T(8,128)S(1)} %bitcast.10), channel_id=1, replica_groups={{0,4,8,12},{16,20,24,28},{1,5,9,13},{17,21,25,29},{2,6,10,14},{18,22,26..., dimensions={0} | all-to-all | bytes 163840 | tf_op jit(solution)/shard_map/all_to_all | solution.py:490
  55.8 1.4 %finish.1 = f32[16,5,16,128]{3,2,1,0:T(8,128)} custom-call(f32[16,5,16,128]{3,2,1,0:T(8,128)S(1)} %get-tuple-element.37.base_ref, f32[16,5,5,16,128]{4,3,2,1,0:T(8,128)S(1)} %get-tuple-element.38.back_ref, f32[16,5,5,16,128]{4,3,2,1,0:T(8,128)S(1)} %get-tuple-element.39.mix_ref, f32[160,128]{1,0:T(8,128)S(1)} %bitcast.9), custom_call_target="tpu_custom_call" | custom-call | flops 6553600 | bytes 1048576 | tf_op jit(solution)/shard_map/finish/pallas_call | solution.py:593
  (1 shorter events, 0.0 us)
Async XLA Ops:
  8.5 6.5 %collective-permute-start = (f32[5,16,128]{2,1,0:T(8,128)S(1)}, f32[5,16,128]{2,1,0:T(8,128)S(1)}, u32[]{:S(2)}, u32[]{:S(2)}) collective-permute-start(f32[5,16,128]{2,1,0:T(8,128)S(1)} %get-tuple-element.32), channel_id=1, source_target_pairs={{0,4},{8,12},{16,20},{24,28},{4,0},{12,8},{20,16},{28,24},{1,5},{9... | collective-permute-start | bytes 122888 | tf_op jit(solution)/shard_map/ppermute | solution.py:482
  11.5 3.4 %collective-permute-start.1 = (f32[5,16,128]{2,1,0:T(8,128)S(1)}, f32[5,16,128]{2,1,0:T(8,128)S(1)}, u32[]{:S(2)}, u32[]{:S(2)}) collective-permute-start(f32[5,16,128]{2,1,0:T(8,128)S(1)} %get-tuple-element.33), channel_id=1, source_target_pairs={{4,8},{12,16},{20,24},{8,4},{16,12},{24,20},{5,9},{13,17},{21,25},... | collective-permute-start | bytes 122888 | tf_op jit(solution)/shard_map/ppermute | solution.py:482
  12.1 4.1 %collective-permute-start.2 = (f32[80,128]{1,0:T(8,128)S(1)}, f32[80,128]{1,0:T(8,128)S(1)}, u32[]{:S(2)}, u32[]{:S(2)}) collective-permute-start(f32[80,128]{1,0:T(8,128)S(1)} %get-tuple-element.34), channel_id=1, source_target_pairs={{0,2},{2,0},{1,3},{3,1},{4,6},{6,4},{5,7},{7,5},{8,10},{10,8},{9,1... | collective-permute-start | bytes 122888 | tf_op jit(solution)/shard_map/ppermute | solution.py:472
  13.7 1.2 %collective-permute-start.3 = (f32[16,128]{1,0:T(8,128)S(1)}, f32[16,128]{1,0:T(8,128)S(1)}, u32[]{:S(2)}, u32[]{:S(2)}) collective-permute-start(f32[16,128]{1,0:T(8,128)S(1)} %get-tuple-element.35), channel_id=1, source_target_pairs={{0,1},{1,0},{2,3},{3,2},{4,5},{5,4},{6,7},{7,6},{8,9},{9,8},{10,11... | collective-permute-start | bytes 24584 | tf_op jit(solution)/shard_map/ppermute | solution.py:472
  37.0 4.9 %collective-permute-start.4 = (f32[24,128]{1,0:T(8,128)S(1)}, f32[24,128]{1,0:T(8,128)S(1)}, u32[]{:S(2)}, u32[]{:S(2)}) collective-permute-start(f32[24,128]{1,0:T(8,128)S(1)} %ahead.1), channel_id=1, source_target_pairs={{0,16},{4,20},{8,24},{12,28},{1,17},{5,21},{9,25},{13,29},{2,18},{... | collective-permute-start | bytes 36872 | tf_op jit(solution)/shard_map/ppermute | solution.py:508
  41.9 6.5 %collective-permute-start.5 = (f32[24,128]{1,0:T(8,128)S(1)}, f32[24,128]{1,0:T(8,128)S(1)}, u32[]{:S(2)}, u32[]{:S(2)}) collective-permute-start(f32[24,128]{1,0:T(8,128)S(1)} %behind.2), channel_id=1, source_target_pairs={{16,0},{20,4},{24,8},{28,12},{17,1},{21,5},{25,9},{29,13},{18,2},{... | collective-permute-start | bytes 36872 | tf_op jit(solution)/shard_map/ppermute | solution.py:522

commit v5 on v4

--- a/solution.py
+++ b/solution.py
@@ -418,6 +418,99 @@
             out_ref[start : start + rows, :] = value
 
 
+def put(sizes, ref, first, values):
+    rows = sizes.rows
+    for i, value in enumerate(values):
+        ref[(first + i) * rows : (first + i + 1) * rows, :] = value
+
+
+def got(sizes, ref, first, count):
+    rows = sizes.rows
+    return [ref[i * rows : (i + 1) * rows, :] for i in range(first, first + count)]
+
+
+STEP = 24
+
+
+def lowered(matrix, power):
+    largest = functools.reduce(jnp.maximum, [jnp.abs(entry) for row in matrix for entry in row])
+    scale, steps = jnp.ones_like(largest), jnp.zeros_like(largest)
+    for i in range(1, 5):
+        big = largest > 2.0 ** (STEP * i)
+        scale = jnp.where(big, 2.0 ** (-STEP * i), scale)
+        steps = jnp.where(big, float(i), steps)
+    return [[entry * scale for entry in row] for row in matrix], power + steps
+
+
+def downscale(steps):
+    scale = jnp.ones_like(steps)
+    for i in range(1, 6):
+        scale = jnp.where(steps >= float(i), 2.0 ** (-STEP * i), scale)
+    return scale
+
+
+def times(left, right):
+    span = range(len(left))
+    return [[combine(left[a][b] * right[b][c] for b in span) for c in span] for a in span]
+
+
+def meet_kernel(sizes, maps_ref, out_ref):
+    comps, rows, square = sizes.comps, sizes.rows, sizes.square
+    span = range(comps)
+    zero = jnp.zeros((rows, LANES), jnp.float32)
+    ahead, behind = chain(sizes, maps_ref)
+    entering, forward = ahead([zero] * comps)
+    unused, backward = behind([zero] * comps, entering)
+
+    def matrix(part, which):
+        start = part * sizes.chunk + (sizes.vectors + which * square) * rows
+        at = lambda i: maps_ref[start + i * rows : start + (i + 1) * rows, :]
+        return [[at(a * comps + b) for b in span] for a in span]
+
+    steps, power = [None], zero
+    for part in range(sizes.group - 1):
+        ahead_map = matrix(part, 0)
+        product = ahead_map if part == 0 else times(ahead_map, steps[-1][0])
+        steps.append(lowered(product, steps[-1][1] if part else zero))
+    total = None
+    for part in reversed(range(sizes.group)):
+        mixed, mixed_power = lowered(matrix(part, 2), zero + 1.0)
+        if part:
+            mixed = times(mixed, steps[part][0])
+            mixed_power = mixed_power + steps[part][1]
+        if total is not None:
+            moved, moved_power = lowered(times(matrix(part, 1), total), power)
+            highest = jnp.maximum(moved_power, mixed_power)
+            one, two = downscale(highest - moved_power), downscale(highest - mixed_power)
+            mixed = [[moved[a][b] * one + mixed[a][b] * two for b in span] for a in span]
+            mixed_power = highest
+        total, power = lowered(mixed, mixed_power)
+    left = lax.axis_index("gx") < sizes.group
+    put(sizes, out_ref, 0, [jnp.where(left, forward[a], backward[a]) for a in span])
+    put(sizes, out_ref, comps, [total[a][b] for a in span for b in span])
+    put(sizes, out_ref, comps + square, [power])
+
+
+def settle_kernel(sizes, maps_ref, own_ref, other_ref, out_ref):
+    comps, rows, square = sizes.comps, sizes.rows, sizes.square
+    span = range(comps)
+    left = lax.axis_index("gx") < sizes.group
+    own, other = got(sizes, own_ref, 0, comps), got(sizes, other_ref, 0, comps)
+    response = got(sizes, other_ref, comps, square)
+    (power,) = got(sizes, other_ref, comps + square, 1)
+    mixed = [combine(response[a * comps + b] * own[b] for b in span) for a in span]
+    for i in range(12):
+        more = power > float(i)
+        mixed = [jnp.where(more, value * 2.0**STEP, value) for value in mixed]
+    ahead, behind = chain(sizes, maps_ref)
+    forward, unused = ahead([jnp.where(left, 0.0, other[a]) for a in span])
+    backward, unused = behind([jnp.where(left, other[a] + mixed[a], 0.0) for a in span], forward)
+    for part in range(sizes.group):
+        for i, value in enumerate(forward[part] + backward[part]):
+            start = part * sizes.vec_rows + i * rows
+            out_ref[start : start + rows, :] = value
+
+
 def finish_kernel(sizes, base_ref, back_ref, mix_ref, vec_ref, update_hbm, update_ref, sems):
     comps, nx = sizes.comps, sizes.nx
     span = range(comps)
@@ -491,6 +584,22 @@
         blocks, "gx", split_axis=0, concat_axis=0, tiled=True, axis_index_groups=groups
     )
     return moved.reshape(array.shape)
+
+
+def solve_pair(sizes, maps):
+    count = sizes.comps + sizes.square + 1
+    rows = round_up(count * sizes.rows, SUB)
+    flops = 1500 * sizes.group * sizes.rows * LANES
+    (leaving,) = call(
+        functools.partial(meet_kernel, sizes), "meet", [VMEM], [floats((rows, LANES))], [], 4, flops
+    )(maps)
+    across = [(i, (i + sizes.group) % sizes.parts) for i in range(sizes.parts)]
+    arrived = lax.ppermute(leaving, "gx", across)
+    (entering,) = call(
+        functools.partial(settle_kernel, sizes), "settle", [VMEM] * 3,
+        [floats((sizes.group * sizes.vec_rows, LANES))], [], 4, flops,
+    )(maps, leaving, arrived)
+    return entering
 
 
 def solve_chain(sizes, maps):
@@ -589,7 +698,8 @@
         from_inner, from_outer, from_south, from_north, from_below, from_above, maps,
     )
     maps = spread(sizes, maps, sizes.chunk)
-    incoming = spread(sizes, solve_chain(sizes, maps), sizes.vec_rows)
+    solve = solve_pair if parts == 2 * sizes.group else solve_chain
+    incoming = spread(sizes, solve(sizes, maps), sizes.vec_rows)
     (update,) = call(
         functools.partial(finish_kernel, sizes), "finish", [VMEM] * 4,
         [floats(state.shape)],

time: 57.4 us -> 52.3 us (0.911)
  starting transfers between devices: 10 us -> 6.91 us
  waiting for transfers between devices: 9.05 us -> 6.77 us
    ppermute x2 -> x1, starting transfers between devices: 4.77 us -> 1.64 us  [solve_pair(): arrived = lax.ppermute(leaving, 'gx', across)]
    ppermute x2 -> x1, waiting for transfers between devices: 6.57 us -> 4.29 us  [solve_pair(): arrived = lax.ppermute(leaving, 'gx', across)]
  transfers between devices with their start and end apart: 6 -> 5, of which waited for: 4 -> 3; matrix products, arithmetic and copies ran while one was open for 0% -> 0% of each run, Pallas kernels for 0% -> 0%
where the time goes in v5:
time: 52.3 us; the launch traced here: 52.1 us
  blocking collectives  23.3 us (45%)
  Pallas kernels  14.4 us (28%)
  starting transfers between devices  6.91 us (13%)
  waiting for transfers between devices  6.77 us (13%)
  between operations  0.67 us (1%)
    all_to_all x2, blocking collectives, spread(): lax.all_to_all(blocks, 'gx', split_axis=0, concat_axis=0, tiled=True, axi...  23.3 us
    pallas_call x1, Pallas kernels, on_device(): call(functools.partial(maps_kernel, sizes), 'maps', [HBM] * len(operands)...  7.52 us
    pallas_call x1, Pallas kernels, on_device(): call(functools.partial(residual_kernel, sizes, gy_two, gz_two), 'residual...  4.63 us
    ppermute x1, waiting for transfers between devices, solve_pair(): arrived = lax.ppermute(leaving, 'gx', across)  4.29 us
    ppermute x1, starting transfers between devices, swapped(): lax.ppermute(inner, 'gx', both(0))  3.03 us
    ppermute x2, waiting for transfers between devices, shifted(): other = lax.ppermute(low, axis, [(0, 1), (1, 0)])  2.47 us
    ppermute x1, starting transfers between devices, solve_pair(): arrived = lax.ppermute(leaving, 'gx', across)  1.64 us
    ppermute x2, starting transfers between devices, shifted(): other = lax.ppermute(low, axis, [(0, 1), (1, 0)])  1.59 us
  transfers between devices with their start and end apart: 5, of which 3 were waited for; matrix products, arithmetic and copies ran while one was open for 0% of the time, Pallas kernels for 0%

profile of v5, /device:TPU:0, one launch (start us, length us, event | category | flops | bytes accessed | tf_op | source)
XLA Modules:
  0.0 52.1 jit_solution(10425428318966214644)
XLA Ops:
  0.6 7.5 %maps.1 = (f32[1376,128]{1,0:T(8,128)S(1)}, f32[16,5,5,16,128]{4,3,2,1,0:T(8,128)S(1)}, f32[16,5,5,16,128]{4,3,2,1,0:T(8,128)S(1)}, f32[16,5,5,16,128]{4,3,2,1,0...) custom-call(f32[16,5,5,16,128]{4,3,2,1,0:T(8,128)} %diag_hbm.1, ...), custom_call_target="tpu_custom_call" | custom-call | flops 37683200 | bytes 1048576 | tf_op jit(solution)/shard_map/maps/pallas_call | solution.py:656
  8.2 0.3 edges.1
  8.5 3.0 %collective-permute-start = (f32[5,16,128]{2,1,0:T(8,128)S(1)}, f32[5,16,128]{2,1,0:T(8,128)S(1)}, u32[]{:S(2)}, u32[]{:S(2)}) collective-permute-start(f32[5,16,128]{2,1,0:T(8,128)S(1)} %get-tuple-element.32), channel_id=1, source_target_pairs={{0,4},{8,12},{16,20},{24,28},{4,0},{12,8},{20,16},{28,24},{1,5},{9... | collective-permute-start | bytes 122888 | tf_op jit(solution)/shard_map/ppermute | solution.py:575
  11.5 0.7 %collective-permute-start.1 = (f32[5,16,128]{2,1,0:T(8,128)S(1)}, f32[5,16,128]{2,1,0:T(8,128)S(1)}, u32[]{:S(2)}, u32[]{:S(2)}) collective-permute-start(f32[5,16,128]{2,1,0:T(8,128)S(1)} %get-tuple-element.33), channel_id=1, source_target_pairs={{4,8},{12,16},{20,24},{8,4},{16,12},{24,20},{5,9},{13,17},{21,25},... | collective-permute-start | bytes 122888 | tf_op jit(solution)/shard_map/ppermute | solution.py:575
  12.1 1.6 %collective-permute-start.2 = (f32[80,128]{1,0:T(8,128)S(1)}, f32[80,128]{1,0:T(8,128)S(1)}, u32[]{:S(2)}, u32[]{:S(2)}) collective-permute-start(f32[80,128]{1,0:T(8,128)S(1)} %get-tuple-element.34), channel_id=1, source_target_pairs={{0,2},{2,0},{1,3},{3,1},{4,6},{6,4},{5,7},{7,5},{8,10},{10,8},{9,1... | collective-permute-start | bytes 122888 | tf_op jit(solution)/shard_map/ppermute | solution.py:565
  13.7 0.0 collective-permute-start.3
  13.7 1.2 %collective-permute-done.3.below_ref.above_ref = f32[16,128]{1,0:T(8,128)S(1)} collective-permute-done((f32[16,128]{1,0:T(8,128)S(1)}, f32[16,128]{1,0:T(8,128)S(1)}, u32[]{:S(2)}, u32[]{:S(2)}) %collective-permute-start.3) | collective-permute-done | bytes 8224 | tf_op jit(solution)/shard_map/ppermute | solution.py:565
  14.9 0.0 collective-permute-done.inner_ref
  14.9 0.0 collective-permute-done.1.outer_ref
  14.9 1.3 %collective-permute-done.2.south_ref.north_ref = f32[80,128]{1,0:T(8,128)S(1)} collective-permute-done((f32[80,128]{1,0:T(8,128)S(1)}, f32[80,128]{1,0:T(8,128)S(1)}, u32[]{:S(2)}, u32[]{:S(2)}) %collective-permute-start.2) | collective-permute-done | bytes 40992 | tf_op jit(solution)/shard_map/ppermute | solution.py:565
  16.2 4.6 %residual.1 = (f32[16,5,16,128]{3,2,1,0:T(8,128)}, f32[16,5,16,128]{3,2,1,0:T(8,128)S(1)}, f32[1376,128]{1,0:T(8,128)S(1)}) custom-call(f32[16,5,16,128]{3,2,1,0:T(8,128)S(1)} %get-tuple-element.22.state_ref, f32[16,5,16,128]{3,2,1,0:T(8,128)S(1)} %get-tuple-element.24.masked_ref, ...), custom_call_target="tpu_custom_call", output_to_operand_aliasing={{2}: (16, {})} | custom-call | flops 21299200 | bytes 1048576 | tf_op jit(solution)/shard_map/residual/pallas_call | solution.py:685
  20.9 16.1 %all_to_all.10 = f32[4,344,128]{2,1,0:T(8,128)S(1)} all-to-all(f32[4,344,128]{2,1,0:T(8,128)S(1)} %bitcast.7), channel_id=1, replica_groups={{0,4,8,12},{16,20,24,28},{1,5,9,13},{17,21,25,29},{2,6,10,14},{18,22,26..., dimensions={0} | all-to-all | bytes 1409024 | tf_op jit(solution)/shard_map/all_to_all | solution.py:583
  36.9 0.5 meet.1.own_ref
  37.4 1.6 %collective-permute-start.4 = (f32[128,128]{1,0:T(8,128)S(1)}, f32[128,128]{1,0:T(8,128)S(1)}, u32[]{:S(2)}, u32[]{:S(2)}) collective-permute-start(f32[128,128]{1,0:T(8,128)S(1)} %meet.1.own_ref), channel_id=1, source_target_pairs={{0,16},{4,20},{8,24},{12,28},{16,0},{20,4},{24,8},{28,12},{1,17},{... | collective-permute-start | bytes 196616 | tf_op jit(solution)/shard_map/ppermute | solution.py:597
  39.1 4.3 %collective-permute-done.4.other_ref = f32[128,128]{1,0:T(8,128)S(1)} collective-permute-done((f32[128,128]{1,0:T(8,128)S(1)}, f32[128,128]{1,0:T(8,128)S(1)}, u32[]{:S(2)}, u32[]{:S(2)}) %collective-permute-start.4) | collective-permute-done | bytes 65568 | tf_op jit(solution)/shard_map/ppermute | solution.py:597
  43.3 0.1 settle.1
  43.4 7.3 %all_to_all.11 = f32[4,40,128]{2,1,0:T(8,128)S(1)} all-to-all(f32[4,40,128]{2,1,0:T(8,128)S(1)} %bitcast.9), channel_id=1, replica_groups={{0,4,8,12},{16,20,24,28},{1,5,9,13},{17,21,25,29},{2,6,10,14},{18,22,26..., dimensions={0} | all-to-all | bytes 163840 | tf_op jit(solution)/shard_map/all_to_all | solution.py:583
  50.7 1.4 %finish.1 = f32[16,5,16,128]{3,2,1,0:T(8,128)} custom-call(f32[16,5,16,128]{3,2,1,0:T(8,128)S(1)} %get-tuple-element.37.base_ref, f32[16,5,5,16,128]{4,3,2,1,0:T(8,128)S(1)} %get-tuple-element.38.back_ref, f32[16,5,5,16,128]{4,3,2,1,0:T(8,128)S(1)} %get-tuple-element.39.mix_ref, f32[160,128]{1,0:T(8,128)S(1)} %bitcast.8), custom_call_target="tpu_custom_call" | custom-call | flops 6553600 | bytes 1048576 | tf_op jit(solution)/shard_map/finish/pallas_call | solution.py:703
Async XLA Ops:
  8.5 6.5 %collective-permute-start = (f32[5,16,128]{2,1,0:T(8,128)S(1)}, f32[5,16,128]{2,1,0:T(8,128)S(1)}, u32[]{:S(2)}, u32[]{:S(2)}) collective-permute-start(f32[5,16,128]{2,1,0:T(8,128)S(1)} %get-tuple-element.32), channel_id=1, source_target_pairs={{0,4},{8,12},{16,20},{24,28},{4,0},{12,8},{20,16},{28,24},{1,5},{9... | collective-permute-start | bytes 122888 | tf_op jit(solution)/shard_map/ppermute | solution.py:575
  11.5 3.4 %collective-permute-start.1 = (f32[5,16,128]{2,1,0:T(8,128)S(1)}, f32[5,16,128]{2,1,0:T(8,128)S(1)}, u32[]{:S(2)}, u32[]{:S(2)}) collective-permute-start(f32[5,16,128]{2,1,0:T(8,128)S(1)} %get-tuple-element.33), channel_id=1, source_target_pairs={{4,8},{12,16},{20,24},{8,4},{16,12},{24,20},{5,9},{13,17},{21,25},... | collective-permute-start | bytes 122888 | tf_op jit(solution)/shard_map/ppermute | solution.py:575
  12.1 4.1 %collective-permute-start.2 = (f32[80,128]{1,0:T(8,128)S(1)}, f32[80,128]{1,0:T(8,128)S(1)}, u32[]{:S(2)}, u32[]{:S(2)}) collective-permute-start(f32[80,128]{1,0:T(8,128)S(1)} %get-tuple-element.34), channel_id=1, source_target_pairs={{0,2},{2,0},{1,3},{3,1},{4,6},{6,4},{5,7},{7,5},{8,10},{10,8},{9,1... | collective-permute-start | bytes 122888 | tf_op jit(solution)/shard_map/ppermute | solution.py:565
  13.7 1.2 %collective-permute-start.3 = (f32[16,128]{1,0:T(8,128)S(1)}, f32[16,128]{1,0:T(8,128)S(1)}, u32[]{:S(2)}, u32[]{:S(2)}) collective-permute-start(f32[16,128]{1,0:T(8,128)S(1)} %get-tuple-element.35), channel_id=1, source_target_pairs={{0,1},{1,0},{2,3},{3,2},{4,5},{5,4},{6,7},{7,6},{8,9},{9,8},{10,11... | collective-permute-start | bytes 24584 | tf_op jit(solution)/shard_map/ppermute | solution.py:565
  37.4 5.9 %collective-permute-start.4 = (f32[128,128]{1,0:T(8,128)S(1)}, f32[128,128]{1,0:T(8,128)S(1)}, u32[]{:S(2)}, u32[]{:S(2)}) collective-permute-start(f32[128,128]{1,0:T(8,128)S(1)} %meet.1.own_ref), channel_id=1, source_target_pairs={{0,16},{4,20},{8,24},{12,28},{16,0},{20,4},{24,8},{28,12},{1,17},{... | collective-permute-start | bytes 196616 | tf_op jit(solution)/shard_map/ppermute | solution.py:597
